TPU v7x, 1024 devices: a whole 4x4x32 slice. The times are simulated.
1024 devices in a mesh: grp: 16 (over y, x), sub: 64 (over z, core).
Axes of the slice: x: 4, y: 4, z: 32, core: 2. Of those that a mesh axis runs over, the one named last changes fastest.
Arguments:
- populations: float32 [19, 128, 128, 384], P(None, 'sub', 'grp')
- heat_pops: float32 [7, 128, 128, 384], P(None, 'sub', 'grp')
- solid_frac: float32 [128, 128, 384], P('sub', 'grp'), may hold values from 0 to 0.5
- coupled_grid_point: int32 [16, 32768], P('grp', 'sub'), may hold values from 0 to 6143
- dest_index: int32 [16, 32768, 1], P('grp', 'sub'), may hold values from 0 to 63; in each aligned block of 512 rows (0 to 511, 512 to 1023, ..., all dimensions but the last counted through in order) at most 16 rows name the same one
- heat_coeff: float32 [16, 32768], P('grp', 'sub'), may hold values from 0.5 to 2
- slot_node: int32 [16, 65536], P('grp', 'sub'), may hold values from 0 to 1023
- node_diag: float32 [16, 512, 128], P('grp', 'sub'), may hold values from 2.5 to 5
- coupling: float32 [16, 512, 128, 128], P('grp', 'sub'), may hold values from 0 to 0.0078125
- block_pattern: int32 [16, 512], P('grp', 'sub'), may hold values from 0 to 7, as said below
- heat_source: float32 [16, 512, 128], P('grp', 'sub')
- solid_start: float32 [16, 512, 128], P('grp', 'sub'), may hold values from -6 to 6
Outputs:
- gas_hotness_after: float32 [128, 128, 384], P('sub', 'grp')
- gas_motion_amount: float32 [3, 128, 128, 384], P(None, 'sub', 'grp')
- solid_temp: float32 [16, 512, 128], P('grp', 'sub')
- fibre_surface_hotness: float32 [16, 32768], P('grp', 'sub')
Inputs may be any that keep to these rules, and one draw needn't show every extreme that they name: `dest_index`: among one device's rows, no owner is named by more than 16 rows, a bound that some block reaches. `block_pattern`: on each device, block b's partner is (b + t) mod 8 for one shift t of 0 to 7 of that device, so every block is the partner of exactly one block.
All inputs are finite; a program needn't handle non-finite values.
Results may differ from a plain program's by a relative error of at most 0.0003.
Values sent between devices are 32-bit elements; how exact they have to be, the bound alone decides.
A program may use at most 64 MiB of HBM per device.

v0:
```python
import functools

import jax
import jax.numpy as jnp
import numpy as np
from jax import lax
from jax.sharding import Mesh
from jax.sharding import PartitionSpec as P

STEPS = 2
ITERS = 2
GRP_SUB = ("grp_0", "grp_1", "sub_0", "sub_1")
GRP = ("grp_0", "grp_1")
SUB = ("sub_0", "sub_1")


flow_velocity = np.array(
    [
        [0, 0, 0],
        [1, 0, 0],
        [-1, 0, 0],
        [0, 1, 0],
        [0, -1, 0],
        [0, 0, 1],
        [0, 0, -1],
        [1, 1, 0],
        [-1, -1, 0],
        [1, -1, 0],
        [-1, 1, 0],
        [1, 0, 1],
        [-1, 0, -1],
        [1, 0, -1],
        [-1, 0, 1],
        [0, 1, 1],
        [0, -1, -1],
        [0, 1, -1],
        [0, -1, 1],
    ],
    dtype=np.int32,
)
flow_weight = np.array([1.0 / 3.0] + [1.0 / 18.0] * 6 + [1.0 / 36.0] * 12)
flow_opposite = np.array(
    [0, 2, 1, 4, 3, 6, 5, 8, 7, 10, 9, 12, 11, 14, 13, 16, 15, 18, 17], dtype=np.int32
)
heat_velocity = flow_velocity[:7]
every_velocity = np.concatenate([flow_velocity, heat_velocity], axis=0)
heat_weight = np.array([0.25] + [0.125] * 6)
tau_flow = 0.8
tau_heat = 0.7
highest = lax.Precision.HIGHEST


def by_axis(shard, axes):
    return functools.reduce(lax.psum, axes, shard)


def with_halo(block, sides, width):
    for axis, dim in sides:
        count = lax.axis_size(axis)
        forward = [(i, i + 1) for i in range(count - 1)]
        forward.append((count - 1, 0))
        backward = [(target, source) for source, target in forward]
        low = lax.ppermute(
            lax.slice_in_dim(block, block.shape[dim] - width, None, axis=dim), axis, forward
        )
        high = lax.ppermute(lax.slice_in_dim(block, 0, width, axis=dim), axis, backward)
        block = jnp.concatenate([low, block, high], axis=dim)
    return block


def sent_together(arrays, axis, split_dim, concat_dim, along):
    ends, at = ([], 0)
    for a in arrays[:-1]:
        at += a.shape[along]
        ends.append(at)
    both = jnp.concatenate(arrays, axis=along)
    return tuple(
        jnp.split(
            lax.all_to_all(both, axis, split_axis=split_dim, concat_axis=concat_dim, tiled=True),
            ends,
            axis=along,
        )
    )


def flow_moments(flow):
    lattice = jnp.asarray(flow_velocity, jnp.float32)
    return jnp.tensordot(lattice, flow, axes=(0, 0), precision=highest)


def collide(flow, caloric_population, solidity):
    lattice = jnp.asarray(flow_velocity, jnp.float32)
    density = jnp.sum(flow, axis=0)
    velocity_field = flow_moments(flow) / density
    speed_square = jnp.sum(velocity_field * velocity_field, axis=0)
    projected = jnp.tensordot(lattice, velocity_field, axes=(1, 0), precision=highest)
    weights = jnp.asarray(flow_weight, jnp.float32)[:, None, None, None]
    balance = (
        weights
        * density
        * (1.0 + 3.0 * projected + 4.5 * projected * projected - 1.5 * speed_square)
    )
    flow_post = (1.0 - solidity) * (flow - (flow - balance) / tau_flow) + solidity * flow[
        flow_opposite
    ]
    stream_hotness = jnp.sum(caloric_population, axis=0)
    heat_lattice = jnp.asarray(heat_velocity, jnp.float32)
    caloric_moment_reduce = jnp.tensordot(
        heat_lattice, velocity_field, axes=(1, 0), precision=highest
    )
    caloric_stencil_shares = jnp.asarray(heat_weight, jnp.float32)[:, None, None, None]
    conserved_power_ledger = (
        caloric_stencil_shares * stream_hotness * (1.0 + 4.0 * caloric_moment_reduce)
    )
    heat_post = caloric_population - (caloric_population - conserved_power_ledger) / tau_heat
    return (flow_post, heat_post)


def stream_margin(padded):
    layers = padded.shape[1]
    across = padded.shape[2]
    lanes = []
    for lane in range(padded.shape[0]):
        step_x, step_y, step_z = every_velocity[lane]
        piece = padded[lane, 1 - step_z : layers - 1 - step_z, 1 - step_x : across - 1 - step_x]
        lanes.append(jnp.roll(piece, int(step_y), axis=2))
    return jnp.stack(lanes)


def apply_solid(vector, diagonal, blocks, picker):
    partner = jnp.dot(picker, vector, precision=highest)
    forward = jnp.einsum("bij,bj->bi", blocks, partner, precision=highest)
    backward_terms = jnp.einsum("bji,bj->bi", blocks, vector, precision=highest)
    backward = jnp.dot(picker.T, backward_terms, precision=highest)
    return diagonal * vector - forward - backward


def paired_totals(first, second):
    return (by_axis(jnp.sum(first * first), GRP_SUB), by_axis(jnp.sum(first * second), GRP_SUB))


def body(
    populations,
    heat_pops,
    solid_frac,
    coupled_grid_point,
    dest_index,
    heat_coeff,
    slot_node,
    node_diag,
    coupling,
    block_pattern,
    heat_source,
    solid_start,
):
    flow = populations
    caloric_population = heat_pops
    for step in range(STEPS):
        flow_post, heat_post = collide(flow, caloric_population, solid_frac)
        joined = jnp.concatenate([flow_post, heat_post], axis=0)
        padded = with_halo(joined, ((GRP, 2), (SUB, 1)), 1)
        passed = stream_margin(padded)
        flow = passed[:19]
        caloric_population = passed[19:]
    stream_hotness = jnp.sum(caloric_population, axis=0)
    gas_motion_amount = flow_moments(flow)
    slabs = lax.axis_size(SUB)
    capacity = slot_node.shape[1] // slabs
    coupling_conductivities = heat_coeff[0]
    interface_flux_rows = (
        coupling_conductivities * stream_hotness.reshape(-1)[coupled_grid_point[0]]
    )
    aimed_entry = dest_index[0, :, 0]
    member = (aimed_entry[:, None] == jnp.arange(slabs, dtype=jnp.int32)[None, :]).astype(jnp.int32)
    current_place = jnp.sum((jnp.cumsum(member, axis=0) - member) * member, axis=1)
    opening_ordinal = aimed_entry * capacity + current_place
    send_flux = (
        jnp.zeros((slabs * capacity,), jnp.float32)
        .at[opening_ordinal]
        .set(interface_flux_rows)
        .reshape(slabs, capacity)
    )
    send_coeff = (
        jnp.zeros((slabs * capacity,), jnp.float32)
        .at[opening_ordinal]
        .set(coupling_conductivities)
        .reshape(slabs, capacity)
    )
    recv_flux, recv_coeff = sent_together((send_flux, send_coeff), SUB, 0, 0, 1)
    node_index = slot_node[0]
    blocks_here = node_diag.shape[1]
    node_count = blocks_here * node_diag.shape[2]
    added_source = jnp.zeros((node_count,), jnp.float32).at[node_index].add(recv_flux.reshape(-1))
    added_diag = jnp.zeros((node_count,), jnp.float32).at[node_index].add(recv_coeff.reshape(-1))
    diagonal = node_diag[0] + added_diag.reshape(node_diag.shape[1:])
    right_side = heat_source[0] + added_source.reshape(node_diag.shape[1:])
    blocks = coupling[0]
    picker = (
        block_pattern[0][:, None] == jnp.arange(blocks_here, dtype=jnp.int32)[None, :]
    ).astype(jnp.float32)
    conduction_approximant = solid_start[0]
    residual = right_side - apply_solid(conduction_approximant, diagonal, blocks, picker)
    image = apply_solid(residual, diagonal, blocks, picker)
    norm_now, product = paired_totals(residual, image)
    step_size = norm_now / product
    direction = residual
    along = image
    for step in range(ITERS):
        conduction_approximant = conduction_approximant + step_size * direction
        if step + 1 < ITERS:
            residual = residual - step_size * along
            image = apply_solid(residual, diagonal, blocks, picker)
            norm_next, product = paired_totals(residual, image)
            growth = norm_next / norm_now
            step_size = norm_next / (product - growth * norm_next / step_size)
            direction = residual + growth * direction
            along = image + growth * along
            norm_now = norm_next
    opening_hotness = conduction_approximant.reshape(-1)[node_index].reshape(slabs, capacity)
    handed_back = lax.all_to_all(opening_hotness, SUB, split_axis=0, concat_axis=0, tiled=True)
    fibre_surface_hotness = handed_back.reshape(-1)[opening_ordinal]
    return (
        stream_hotness,
        gas_motion_amount,
        conduction_approximant[None],
        fibre_surface_hotness[None],
    )


def solution(mesh):
    torus = Mesh(mesh.devices.reshape(4, 4, 32, 2), ("grp_0", "grp_1", "sub_0", "sub_1"))
    return jax.shard_map(
        body,
        mesh=torus,
        in_specs=(
            P(None, SUB, GRP, None),
            P(None, SUB, GRP, None),
            P(SUB, GRP, None),
            P(GRP, SUB),
            P(GRP, SUB, None),
            P(GRP, SUB),
            P(GRP, SUB),
            P(GRP, SUB, None),
            P(GRP, SUB, None, None),
            P(GRP, SUB),
            P(GRP, SUB, None),
            P(GRP, SUB, None),
        ),
        out_specs=(P(SUB, GRP, None), P(None, SUB, GRP, None), P(GRP, SUB, None), P(GRP, SUB)),
        check_vma=False,
    )
```

profile of v0, /device:TPU:1, one launch (start us, length us, event | category | flops | bytes accessed | tf_op | source)
XLA Modules:
  0.0 350.6 jit_solution(233107591795485994)
XLA Ops:
  0.7 1.2 reduce_sum.216
  1.9 1.6 multiply_reduce_fusion.1
  3.6 0.7 fusion.81
  4.7 0.6 pad_clamp_fusion.1
  5.3 0.6 gather_fusion
  6.1 0.5 copy-done.8
  6.9 7.7 %collective-permute-start.1 = (f32[26,2,1,384]{3,2,1,0:T(1,128)S(1)}, f32[26,2,1,384]{3,2,1,0:T(1,128)S(1)}, u32[]{:S(2)}, u32[]{:S(2)}) collective-permute-start(f32[26,2,1,384]{3,2,1,0:T(1,128)S(1)} %get-tuple-element.88), channel_id=1, source_target_pairs={{64,0},{128,64},{192,128},{256,192},{320,256},{384,320},{448,384},... | collective-permute-start | bytes 239624 | tf_op jit(solution)/shard_map/ppermute | solution.py:66
  14.6 1.9 collective-permute-start
  16.6 1.2 reduce-window.6
  18.2 2.6 scatter_custom_fusion.1
  20.8 0.7 reshape.256
  21.7 1.2 fusion.16
  22.9 1.5 fusion.18
  24.4 0.6 pad_clamp_fusion
  25.3 0.4 copy.109
  25.8 10.4 %collective-permute-start.3 = (f32[26,1,10,384]{3,1,2,0:T(1,128)S(1)}, f32[26,1,10,384]{3,1,2,0:T(1,128)S(1)}, u32[]{:S(2)}, u32[]{:S(2)}) collective-permute-start(f32[26,1,10,384]{3,1,2,0:T(1,128)S(1)} %copy.109), channel_id=1, source_target_pairs={{1,0},{2,1},{3,2},{4,3},{5,4},{6,5},{7,6},{8,7},{9,8},{10,9},{11,1... | collective-permute-start | bytes 1198088 | tf_op jit(solution)/shard_map/ppermute | solution.py:66
  36.2 0.4 copy.107
  36.6 0.6 broadcast_clamp_fusion
  37.6 0.6 maximum_bitcast_fusion.4
  38.2 0.7 slice.507
  38.9 5.4 %collective-permute-done.2 = f32[26,1,10,384]{3,1,2,0:T(1,128)S(1)} collective-permute-done((f32[26,1,10,384]{3,1,2,0:T(1,128)S(1)}, f32[26,1,10,384]{3,1,2,0:T(1,128)S(1)}, u32[]{:S(2)}, u32[]{:S(2)}) %collective-permute-start.2) | collective-permute-done | bytes 399392 | tf_op jit(solution)/shard_map/ppermute | solution.py:63
  45.2 0.7 add_bitcast_fusion.1
  46.7 0.7 gather_fusion.1
  47.5 1.4 multiply_reduce_fusion
  48.9 1.0 fusion.82
  49.9 0.7 fusion.83
  50.8 0.7 copy-done.5
  52.2 6.7 %collective-permute-start.5 = (f32[26,2,1,384]{3,2,1,0:T(1,128)S(1)}, f32[26,2,1,384]{3,2,1,0:T(1,128)S(1)}, u32[]{:S(2)}, u32[]{:S(2)}) collective-permute-start(f32[26,2,1,384]{3,2,1,0:T(1,128)S(1)} %get-tuple-element.86), channel_id=1, source_target_pairs={{64,0},{128,64},{192,128},{256,192},{320,256},{384,320},{448,384},... | collective-permute-start | bytes 239624 | tf_op jit(solution)/shard_map/ppermute | solution.py:66
  58.9 2.1 collective-permute-start.4
  61.1 6.4 %collective-permute-done.4 = f32[26,2,1,384]{3,2,1,0:T(1,128)S(1)} collective-permute-done((f32[26,2,1,384]{3,2,1,0:T(1,128)S(1)}, f32[26,2,1,384]{3,2,1,0:T(1,128)S(1)}, u32[]{:S(2)}, u32[]{:S(2)}) %collective-permute-start.4) | collective-permute-done | bytes 79904 | tf_op jit(solution)/shard_map/ppermute | solution.py:63
  68.6 8.7 %collective-permute-start.7 = (f32[26,1,10,384]{3,1,2,0:T(1,128)S(1)}, f32[26,1,10,384]{3,1,2,0:T(1,128)S(1)}, u32[]{:S(2)}, u32[]{:S(2)}) collective-permute-start(f32[26,1,10,384]{3,1,2,0:T(1,128)S(1)} %copy.118), channel_id=1, source_target_pairs={{1,0},{2,1},{3,2},{4,3},{5,4},{6,5},{7,6},{8,7},{9,8},{10,9},{11,1... | collective-permute-start | bytes 1198088 | tf_op jit(solution)/shard_map/ppermute | solution.py:66
  78.2 0.5 collective-permute-done.7
  79.8 0.7 bitcast_add_fusion
  80.6 3.1 gather_fusion.2
  83.8 2.6 scatter_custom_fusion
  86.5 0.7 pad_maximum_fusion.6
  87.2 20.9 %all-to-all-start = ((f32[64,1,32]{2,1,0:T(1,128)}), f32[64,1,32]{2,1,0:T(1,128)S(1)}, u32[]{:S(2)}, u32[]{:S(2)}) async-start(f32[64,1,32]{2,1,0:T(1,128)} %bitcast.74), calls=%async_computation | async-start | bytes 65536 | tf_op jit(solution)/shard_map/all_to_all | solution.py:79
  108.3 22.0 %all-to-all-done = f32[64,1,32]{2,1,0:T(1,128)S(1)} async-done(((f32[64,1,32]{2,1,0:T(1,128)}), f32[64,1,32]{2,1,0:T(1,128)S(1)}, u32[]{:S(2)}, u32[]{:S(2)}) %all-to-all-start) | async-done | bytes 8224 | tf_op jit(solution)/shard_map/all_to_all | solution.py:79
  130.5 7.8 %scatter_custom_fusion.2 = f32[1024]{0:T(1024)S(1)} fusion(s32[1024]{0:T(1024)} %bitcast.386, f32[1024]{0:T(1024)S(1)} %reshape.323, f32[]{:T(128)} %constant.19.clone.1), kind=kCustom, calls=%fused_computation.256 | custom fusion | flops 1024 | bytes 4608 | tf_op jit(solution)/shard_map/scatter-add | solution.py:193
  138.4 7.8 %scatter_custom_fusion.3 = f32[1024]{0:T(1024)S(1)} fusion(s32[1024]{0:T(1024)} %bitcast.387, f32[1024]{0:T(1024)S(1)} %reshape.331, f32[]{:T(128)} %constant.19.clone.1), kind=kCustom, calls=%fused_computation.254 | custom fusion | flops 1024 | bytes 4608 | tf_op jit(solution)/shard_map/scatter-add | solution.py:194
  146.6 0.5 fusion.12
  147.2 0.9 fusion.14
  148.1 0.9 multiply_reduce_fusion.3
  149.0 6.6 %all-reduce.5 = (f32[]{:T(128)}, f32[]{:T(128)}) all-reduce(f32[]{:T(128)} %get-tuple-element.21, f32[]{:T(128)} %get-tuple-element.20), channel_id=1, replica_groups=mesh['grp_0'=4,'grp_1'=4,'sub_0'=32,'sub_1'=2] {'grp_0'}, use_global_device_ids=true, to_apply=%region_12.13 | all-reduce | flops 2 | bytes 16 | tf_op jit(solution)/shard_map/psum | solution.py:54
  155.6 6.6 %all-reduce.3 = (f32[]{:T(128)}, f32[]{:T(128)}) all-reduce(f32[]{:T(128)} %get-tuple-element.32, f32[]{:T(128)} %get-tuple-element.33), channel_id=1, replica_groups=mesh['grp_0'=4,'grp_1'=4,'sub_0'=32,'sub_1'=2] {'grp_1'}, use_global_device_ids=true, to_apply=%region_13.14 | all-reduce | flops 2 | bytes 16 | tf_op jit(solution)/shard_map/psum | solution.py:54
  162.2 40.8 %all-reduce.1 = (f32[]{:T(128)}, f32[]{:T(128)}) all-reduce(f32[]{:T(128)} %get-tuple-element.28, f32[]{:T(128)} %get-tuple-element.29), channel_id=1, replica_groups=mesh['grp_0'=4,'grp_1'=4,'sub_0'=32,'sub_1'=2] {'sub_0'}, use_global_device_ids=true, to_apply=%region_14.15 | all-reduce | flops 2 | bytes 16 | tf_op jit(solution)/shard_map/psum | solution.py:54
  203.0 21.2 %all-reduce.7 = (f32[]{:T(128)}, f32[]{:T(128)}) all-reduce(f32[]{:T(128)} %get-tuple-element.24, f32[]{:T(128)} %get-tuple-element.25), channel_id=1, replica_groups=mesh['grp_0'=4,'grp_1'=4,'sub_0'=32,'sub_1'=2] {'sub_1'}, use_global_device_ids=true, to_apply=%region_15.16 | all-reduce | flops 2 | bytes 16 | tf_op jit(solution)/shard_map/psum | solution.py:54
  225.5 0.6 multiply_reduce_fusion.2
  226.3 0.5 fusion.8
  226.8 0.9 fusion.10
  227.8 0.9 fusion.7
  228.6 8.1 %all-reduce.4 = (f32[]{:T(128)}, f32[]{:T(128)}) all-reduce(f32[]{:T(128)} %get-tuple-element.38, f32[]{:T(128)} %fusion.7), channel_id=1, replica_groups=mesh['grp_0'=4,'grp_1'=4,'sub_0'=32,'sub_1'=2] {'grp_0'}, use_global_device_ids=true, to_apply=%region_22.23 | all-reduce | flops 2 | bytes 16 | tf_op jit(solution)/shard_map/psum | solution.py:54
  236.8 8.3 %all-reduce.2 = (f32[]{:T(128)}, f32[]{:T(128)}) all-reduce(f32[]{:T(128)} %get-tuple-element.30, f32[]{:T(128)} %get-tuple-element.31), channel_id=1, replica_groups=mesh['grp_0'=4,'grp_1'=4,'sub_0'=32,'sub_1'=2] {'grp_1'}, use_global_device_ids=true, to_apply=%region_23.24 | all-reduce | flops 2 | bytes 16 | tf_op jit(solution)/shard_map/psum | solution.py:54
  245.1 40.8 %all-reduce = (f32[]{:T(128)}, f32[]{:T(128)}) all-reduce(f32[]{:T(128)} %get-tuple-element.26, f32[]{:T(128)} %get-tuple-element.27), channel_id=1, replica_groups=mesh['grp_0'=4,'grp_1'=4,'sub_0'=32,'sub_1'=2] {'sub_0'}, use_global_device_ids=true, to_apply=%region_24.25 | all-reduce | flops 2 | bytes 16 | tf_op jit(solution)/shard_map/psum | solution.py:54
  285.9 21.2 %all-reduce.6 = (f32[]{:T(128)}, f32[]{:T(128)}) all-reduce(f32[]{:T(128)} %get-tuple-element.22, f32[]{:T(128)} %get-tuple-element.23), channel_id=1, replica_groups=mesh['grp_0'=4,'grp_1'=4,'sub_0'=32,'sub_1'=2] {'sub_1'}, use_global_device_ids=true, to_apply=%region_25.26 | all-reduce | flops 2 | bytes 16 | tf_op jit(solution)/shard_map/psum | solution.py:54
  311.7 4.5 %gather_fusion.3 = f32[1024]{0:T(1024)S(1)} fusion(f32[1024]{0:T(1024)S(1)} %bitcast.359, s32[1024]{0:T(1024)S(1)} %copy-done.17), kind=kCustom, calls=%fused_computation.3 | custom fusion | bytes 12288 | tf_op jit(solution)/shard_map/gather | solution.py:219
  316.2 0.7 all_to_all.17
  316.9 6.3 %all-to-all-start.1 = ((f32[64,1,16]{2,1,0:T(1,128)}), f32[64,1,16]{2,1,0:T(1,128)S(1)}, u32[]{:S(2)}, u32[]{:S(2)}) async-start(f32[64,1,16]{2,1,0:T(1,128)} %bitcast.107), calls=%async_computation.1 | async-start | bytes 65536 | tf_op jit(solution)/shard_map/all_to_all | solution.py:220
  323.2 0.5 fusion.3
  323.7 0.6 copy.124
  324.4 21.5 %all-to-all-done.1 = f32[64,1,16]{2,1,0:T(1,128)S(1)} async-done(((f32[64,1,16]{2,1,0:T(1,128)}), f32[64,1,16]{2,1,0:T(1,128)S(1)}, u32[]{:S(2)}, u32[]{:S(2)}) %all-to-all-start.1) | async-done | bytes 4128 | tf_op jit(solution)/shard_map/all_to_all | solution.py:220
  345.9 0.5 broadcast.210
  346.4 0.7 reduce.38
  347.2 3.4 gather_fusion.4
  (204 shorter events, 9.1 us)
Async XLA Ops:
  0.6 21.1 %copy-start = (f32[1,8,128,128]{3,2,1,0:T(8,128)S(1)}, f32[1,8,128,128]{3,2,1,0:T(8,128)}, u32[]{:S(2)}) copy-start(f32[1,8,128,128]{3,2,1,0:T(8,128)} %param.34) | copy-start | bytes 1572868
  0.6 2.9 copy-start.13
  0.7 3.6 %copy-start.20 = (f32[7,3,1,1]{0,1,3,2:T(4,128)S(1)}, f32[7,3,1,1]{0,1,3,2:T(4,128)}, u32[]{:S(2)}) copy-start(f32[7,3,1,1]{0,1,3,2:T(4,128)} %constant.74) | copy-start | bytes 256
  0.7 4.0 %copy-start.32 = (s32[19]{0:T(128)S(1)}, s32[19]{0:T(128)}, u32[]{:S(2)}) copy-start(s32[19]{0:T(128)} %constant.71) | copy-start | bytes 232
  0.7 4.6 %copy-start.2 = (f32[19,2,8,384]{3,2,1,0:T(8,128)S(1)}, f32[19,2,8,384]{3,2,1,0:T(8,128)}, u32[]{:S(2)}) copy-start(f32[19,2,8,384]{3,2,1,0:T(8,128)} %param.26) | copy-start | bytes 1400836
  0.7 3.9 %copy-start.3 = (f32[7,2,8,384]{3,2,1,0:T(8,128)S(1)}, f32[7,2,8,384]{3,2,1,0:T(8,128)}, u32[]{:S(2)}) copy-start(f32[7,2,8,384]{3,2,1,0:T(8,128)} %param.27) | copy-start | bytes 516100
  0.7 4.0 %copy-start.31 = (s32[1,512]{1,0:T(1,128)S(1)}, s32[1,512]{1,0:T(1,128)}, u32[]{:S(2)}) copy-start(s32[1,512]{1,0:T(1,128)} %param.29) | copy-start | bytes 6148
  3.5 2.4 copy-start.6
  3.5 2.4 copy-start.28
  3.5 3.0 copy-start.26
  5.3 0.7 copy-start.22
  5.9 0.6 copy-start.8
  6.5 10.0 %copy-start.14 = (s32[1,512,1]{1,2,0:T(1,128)S(1)}, s32[1,512,1]{1,2,0:T(1,128)}, u32[]{:S(2)}) copy-start(s32[1,512,1]{1,2,0:T(1,128)} %param.30) | copy-start | bytes 6148
  6.8 14.7 %copy-start.15 = (f32[1,8,128]{2,1,0:T(8,128)S(1)}, f32[1,8,128]{2,1,0:T(8,128)}, u32[]{:S(2)}) copy-start(f32[1,8,128]{2,1,0:T(8,128)} %param.37) | copy-start | bytes 12292
  6.8 14.7 %copy-start.35 = (s32[1,8]{1,0:T(1,128)S(1)}, s32[1,8]{1,0:T(1,128)}, u32[]{:S(2)}) copy-start(s32[1,8]{1,0:T(1,128)} %param.35) | copy-start | bytes 100
  6.9 18.0 %collective-permute-start.1 = (f32[26,2,1,384]{3,2,1,0:T(1,128)S(1)}, f32[26,2,1,384]{3,2,1,0:T(1,128)S(1)}, u32[]{:S(2)}, u32[]{:S(2)}) collective-permute-start(f32[26,2,1,384]{3,2,1,0:T(1,128)S(1)} %get-tuple-element.88), channel_id=1, source_target_pairs={{64,0},{128,64},{192,128},{256,192},{320,256},{384,320},{448,384},... | collective-permute-start | bytes 239624 | tf_op jit(solution)/shard_map/ppermute | solution.py:66
  14.6 10.4 %collective-permute-start = (f32[26,2,1,384]{3,2,1,0:T(1,128)S(1)}, f32[26,2,1,384]{3,2,1,0:T(1,128)S(1)}, u32[]{:S(2)}, u32[]{:S(2)}) collective-permute-start(f32[26,2,1,384]{3,2,1,0:T(1,128)S(1)} %get-tuple-element.87), channel_id=1, source_target_pairs={{0,64},{64,128},{128,192},{192,256},{256,320},{320,384},{384,448},... | collective-permute-start | bytes 239624 | tf_op jit(solution)/shard_map/ppermute | solution.py:63
  18.2 7.0 %copy-start.21 = (s32[512,1]{0,1:T(1,128)}, s32[512,1]{0,1:T(1,128)S(1)}, u32[]{:S(2)}) copy-start(s32[512,1]{0,1:T(1,128)S(1)} %compare_select_fusion.2) | copy-start | bytes 6148
  25.2 10.9 %copy-start.25 = (s32[1,1024]{1,0:T(1,128)S(1)}, s32[1,1024]{1,0:T(1,128)}, u32[]{:S(2)}) copy-start(s32[1,1024]{1,0:T(1,128)} %param.32) | copy-start | bytes 12292
  25.8 11.8 %collective-permute-start.3 = (f32[26,1,10,384]{3,1,2,0:T(1,128)S(1)}, f32[26,1,10,384]{3,1,2,0:T(1,128)S(1)}, u32[]{:S(2)}, u32[]{:S(2)}) collective-permute-start(f32[26,1,10,384]{3,1,2,0:T(1,128)S(1)} %copy.109), channel_id=1, source_target_pairs={{1,0},{2,1},{3,2},{4,3},{5,4},{6,5},{7,6},{8,7},{9,8},{10,9},{11,1... | collective-permute-start | bytes 1198088 | tf_op jit(solution)/shard_map/ppermute | solution.py:66
  36.2 1.3 copy-start.16
  36.6 7.7 %collective-permute-start.2 = (f32[26,1,10,384]{3,1,2,0:T(1,128)S(1)}, f32[26,1,10,384]{3,1,2,0:T(1,128)S(1)}, u32[]{:S(2)}, u32[]{:S(2)}) collective-permute-start(f32[26,1,10,384]{3,1,2,0:T(1,128)S(1)} %copy.107), channel_id=1, source_target_pairs={{0,1},{1,2},{2,3},{3,4},{4,5},{5,6},{6,7},{7,8},{8,9},{9,10},{10,1... | collective-permute-start | bytes 1198088 | tf_op jit(solution)/shard_map/ppermute | solution.py:63
  47.5 3.2 copy-start.4
  47.5 3.2 copy-start.10
  50.6 0.9 copy-start.5
  50.7 1.0 copy-start.29
  50.7 1.1 copy-start.7
  50.7 1.1 copy-start.9
  50.7 1.1 copy-start.12
  50.7 1.1 copy-start.27
  52.2 8.8 %collective-permute-start.5 = (f32[26,2,1,384]{3,2,1,0:T(1,128)S(1)}, f32[26,2,1,384]{3,2,1,0:T(1,128)S(1)}, u32[]{:S(2)}, u32[]{:S(2)}) collective-permute-start(f32[26,2,1,384]{3,2,1,0:T(1,128)S(1)} %get-tuple-element.86), channel_id=1, source_target_pairs={{64,0},{128,64},{192,128},{256,192},{320,256},{384,320},{448,384},... | collective-permute-start | bytes 239624 | tf_op jit(solution)/shard_map/ppermute | solution.py:66
  58.9 8.5 %collective-permute-start.4 = (f32[26,2,1,384]{3,2,1,0:T(1,128)S(1)}, f32[26,2,1,384]{3,2,1,0:T(1,128)S(1)}, u32[]{:S(2)}, u32[]{:S(2)}) collective-permute-start(f32[26,2,1,384]{3,2,1,0:T(1,128)S(1)} %get-tuple-element.85), channel_id=1, source_target_pairs={{0,64},{64,128},{128,192},{192,256},{256,320},{320,384},{384,448},... | collective-permute-start | bytes 239624 | tf_op jit(solution)/shard_map/ppermute | solution.py:63
  68.2 9.9 %collective-permute-start.6 = (f32[26,1,10,384]{3,1,2,0:T(1,128)S(1)}, f32[26,1,10,384]{3,1,2,0:T(1,128)S(1)}, u32[]{:S(2)}, u32[]{:S(2)}) collective-permute-start(f32[26,1,10,384]{3,1,2,0:T(1,128)S(1)} %copy.116), channel_id=1, source_target_pairs={{0,1},{1,2},{2,3},{3,4},{4,5},{5,6},{6,7},{7,8},{8,9},{9,10},{10,1... | collective-permute-start | bytes 1198088 | tf_op jit(solution)/shard_map/ppermute | solution.py:63
  68.6 10.1 %collective-permute-start.7 = (f32[26,1,10,384]{3,1,2,0:T(1,128)S(1)}, f32[26,1,10,384]{3,1,2,0:T(1,128)S(1)}, u32[]{:S(2)}, u32[]{:S(2)}) collective-permute-start(f32[26,1,10,384]{3,1,2,0:T(1,128)S(1)} %copy.118), channel_id=1, source_target_pairs={{1,0},{2,1},{3,2},{4,3},{5,4},{6,5},{7,6},{8,7},{9,8},{10,9},{11,1... | collective-permute-start | bytes 1198088 | tf_op jit(solution)/shard_map/ppermute | solution.py:66
  79.8 0.8 copy-start.19
  80.5 3.3 copy-start.30
  80.5 6.0 %copy-start.11 = (f32[64,16]{1,0:T(8,128)S(1)}, f32[64,16]{1,0:T(8,128)}, u32[]{:S(2)}) copy-start(f32[64,16]{1,0:T(8,128)} %reshape.256) | copy-start | bytes 12292
  80.6 65.5 %copy-start.23 = (f32[8,1,128]{2,1,0:T(1,128)S(1)}, f32[8,1,128]{2,1,0:T(1,128)}, u32[]{:S(2)}) copy-start(f32[8,1,128]{2,1,0:T(1,128)} %fusion.16) | copy-start | bytes 12292
  80.6 65.5 %copy-start.24 = (f32[8,1,128]{2,1,0:T(1,128)S(1)}, f32[8,1,128]{2,1,0:T(1,128)}, u32[]{:S(2)}) copy-start(f32[8,1,128]{2,1,0:T(1,128)} %fusion.18) | copy-start | bytes 12292
  80.6 65.5 %copy-start.33 = (f32[1,8,128]{2,1,0:T(8,128)S(1)}, f32[1,8,128]{2,1,0:T(8,128)}, u32[]{:S(2)}) copy-start(f32[1,8,128]{2,1,0:T(8,128)} %param.36) | copy-start | bytes 12292
  80.6 65.5 %copy-start.34 = (f32[1,8,128]{2,1,0:T(8,128)S(1)}, f32[1,8,128]{2,1,0:T(8,128)}, u32[]{:S(2)}) copy-start(f32[1,8,128]{2,1,0:T(8,128)} %param.33) | copy-start | bytes 12292
  80.6 65.5 %copy-start.36 = (s32[1,8]{1,0:T(1,128)S(1)}, s32[1,8]{1,0:T(1,128)}, u32[]{:S(2)}) copy-start(s32[1,8]{1,0:T(1,128)} %param.35) | copy-start | bytes 100
  87.2 43.2 %all-to-all-start = ((f32[64,1,32]{2,1,0:T(1,128)}), f32[64,1,32]{2,1,0:T(1,128)S(1)}, u32[]{:S(2)}, u32[]{:S(2)}) async-start(f32[64,1,32]{2,1,0:T(1,128)} %bitcast.74), calls=%async_computation | async-start | bytes 65536 | tf_op jit(solution)/shard_map/all_to_all | solution.py:79
  146.2 165.5 %copy-start.17 = (s32[1024]{0:T(1024)S(1)}, s32[1024]{0:T(1024)}, u32[]{:S(2)}) copy-start(s32[1024]{0:T(1024)} %broadcast_clamp_fusion) | copy-start | bytes 12292
  311.6 4.6 %copy-start.1 = (f32[8,128]{1,0:T(8,128)}, f32[8,128]{1,0:T(8,128)S(1)}, u32[]{:S(2)}) copy-start(f32[8,128]{1,0:T(8,128)S(1)} %fusion.60) | copy-start | bytes 12292
  311.6 35.6 %copy-start.18 = (s32[1024]{0:T(1024)S(1)}, s32[1024]{0:T(1024)}, u32[]{:S(2)}) copy-start(s32[1024]{0:T(1024)} %pad_clamp_fusion) | copy-start | bytes 12292
  316.9 29.0 %all-to-all-start.1 = ((f32[64,1,16]{2,1,0:T(1,128)}), f32[64,1,16]{2,1,0:T(1,128)S(1)}, u32[]{:S(2)}, u32[]{:S(2)}) async-start(f32[64,1,16]{2,1,0:T(1,128)} %bitcast.107), calls=%async_computation.1 | async-start | bytes 65536 | tf_op jit(solution)/shard_map/all_to_all | solution.py:220
where the time goes:
time: 351 us
  blocking collectives  154 us (44%)
  starting transfers between devices  64.6 us (18%)
  waiting for transfers between devices  56.4 us (16%)
  other arithmetic  27.3 us (8%)
  local copies, waits for them, and re-layouts  26.6 us (8%)
  matrix products  14.5 us (4%)
  between operations  7.57 us (2%)
    psum x8, blocking collectives, by_axis(): return functools.reduce(lax.psum, axes, shard)  154 us
    ppermute x4, starting transfers between devices, with_halo(): lax.ppermute(lax.slice_in_dim(block, 0, width, axis=dim), axis, backward)  33.4 us
    all_to_all x1, waiting for transfers between devices, sent_together(): lax.all_to_all(both, axis, split_axis=split_dim, concat_axis=concat_dim,...  22 us
    all_to_all x1, waiting for transfers between devices, body(): lax.all_to_all(opening_hotness, SUB, split_axis=0, concat_axis=0, tiled=T...  21.5 us
    all_to_all x1, starting transfers between devices, sent_together(): lax.all_to_all(both, axis, split_axis=split_dim, concat_axis=concat_dim,...  20.9 us
    scatter-add x2, other arithmetic, body(): jnp.zeros((node_count,), jnp.float32).at[node_index]  15.5 us
    ppermute x4, waiting for transfers between devices, with_halo(): lax.ppermute(lax.slice_in_dim(block, block.shape[dim] - width, None, axis...  12.1 us
  transfers between devices with their start and end apart: 10, of which 7 were waited for; matrix products, arithmetic and copies ran while one was open for 4% of the time, Pallas kernels for 0%

commit v1 on v0

v1 whole, which is shorter than its diff:
```python
import functools

import jax
import jax.numpy as jnp
import numpy as np
from jax import lax
from jax.experimental import pallas as pl
from jax.experimental.pallas import tpu as pltpu
from jax.sharding import PartitionSpec as P

MESH = pl.DeviceIdType.MESH
F32 = jnp.float32
BF16 = jnp.bfloat16
I32 = jnp.int32

STEPS = 2
CY = 384
CAP = 16
SHIFT = 4.0

FLOW = [
    (0, 0, 0),
    (1, 0, 0),
    (-1, 0, 0),
    (0, 1, 0),
    (0, -1, 0),
    (0, 0, 1),
    (0, 0, -1),
    (1, 1, 0),
    (-1, -1, 0),
    (1, -1, 0),
    (-1, 1, 0),
    (1, 0, 1),
    (-1, 0, -1),
    (1, 0, -1),
    (-1, 0, 1),
    (0, 1, 1),
    (0, -1, -1),
    (0, 1, -1),
    (0, -1, 1),
]
EVERY = FLOW + FLOW[:7]
WEIGHT = [1.0 / 3.0] + [1.0 / 18.0] * 6 + [1.0 / 36.0] * 12
HEAT_WEIGHT = [0.25] + [0.125] * 6
TAU_FLOW = 0.8
TAU_HEAT = 0.7

X_UP = [i for i, e in enumerate(EVERY) if e[0] == 1]
X_DOWN = [i for i, e in enumerate(EVERY) if e[0] == -1]
Z_UP = [i for i, e in enumerate(EVERY) if e[2] == 1]
Z_DOWN = [i for i, e in enumerate(EVERY) if e[2] == -1]
EDGES = [
    next(i for i, e in enumerate(FLOW) if e == (1, 0, 1)),
    next(i for i, e in enumerate(FLOW) if e == (-1, 0, 1)),
    next(i for i, e in enumerate(FLOW) if e == (1, 0, -1)),
    next(i for i, e in enumerate(FLOW) if e == (-1, 0, -1)),
]


def dot(a, b, dims):
    return lax.dot_general(a, b, (dims, ((), ())), preferred_element_type=F32)


def parts3(v):
    a = v.astype(BF16).astype(F32)
    rest = v - a
    b = rest.astype(BF16).astype(F32)
    return a, b, rest - b


def iota(shape, dim):
    return lax.broadcasted_iota(I32, shape, dim)


def total(v):
    return jnp.sum(jnp.sum(v, axis=1, keepdims=True), axis=0, keepdims=True)


def kernel(
    groups,
    bands,
    pops_ref,
    heat_ref,
    solid_ref,
    voxel_ref,
    dest_ref,
    coeff_ref,
    slot_ref,
    diag_ref,
    coup_ref,
    pat_ref,
    source_ref,
    start_ref,
    temp_out,
    motion_out,
    solid_out,
    rows_out,
    cur,
    post,
    zs,
    zr,
    xs,
    xr,
    er,
    chop,
    cthop,
    lohot,
    mask,
    place,
    dhot,
    lo_vox,
    ecode,
    fcode,
    send1,
    recv1,
    send2,
    recv2,
    back1,
    rback1,
    back2,
    rback2,
    tot,
    rtot,
    halo_send,
    halo_recv,
    sems_send,
    sems_recv,
    grp_send,
    grp_recv,
):
    subs = groups * 8
    gi = lax.axis_index("grp")
    si = lax.axis_index("sub")
    g = si // 8
    j = si % 8
    g_up = lax.rem(gi + 1, bands)
    g_dn = lax.rem(gi + bands - 1, bands)
    s_up = lax.rem(si + 1, subs)
    s_dn = lax.rem(si + subs - 1, subs)

    barrier = pltpu.get_barrier_semaphore()

    def greet(a, b):
        pl.semaphore_signal(barrier, inc=1, device_id=(a, b), device_id_type=MESH)

    for a, b in (
        (gi, s_up),
        (gi, s_dn),
        (g_up, si),
        (g_dn, si),
        (g_up, s_up),
        (g_up, s_dn),
        (g_dn, s_up),
        (g_dn, s_dn),
    ):
        greet(a, b)

    def greet_strip(i, carry):
        greet(gi, lax.rem(g + i, groups) * 8 + j)
        greet(gi, g * 8 + lax.rem(j + i, 8))
        return carry

    lax.fori_loop(1, 8, greet_strip, 0)

    def greet_bands(i, carry):
        greet(lax.rem(gi + i, bands), si)
        return carry

    lax.fori_loop(1, bands, greet_bands, 0)

    cur[0:19] = pops_ref[...]
    cur[19:26] = heat_ref[...]
    xs[:, :, 8:16] = jnp.zeros((STEPS, 2, 8, CY), F32)

    for b in range(8):
        block = coup_ref[0, b]
        high = block.astype(BF16).astype(F32)
        low = block - high
        rows = pl.ds(b * 128, 128)
        chop[rows, 0:128] = high.astype(BF16)
        chop[rows, 128:256] = low.astype(BF16)
        cthop[rows, 0:128] = high.T.astype(BF16)
        cthop[rows, 128:256] = low.T.astype(BF16)

    wide = 16 * 128
    a_of = iota((128, wide), 0)
    c_of = iota((128, wide), 1)
    k_of = c_of // 128
    lane_of = c_of % 128
    p_of = lane_of // 32
    t_of = (lane_of // 8) % 4
    ecode[...] = jnp.where(
        (a_of == p_of * 32 + t_of * 16 + k_of) & (p_of < 3) & (t_of < 2), 1.0, 0.0
    ).astype(BF16)
    spread = jnp.where(a_of == k_of, 1.0, 0.0).astype(BF16)
    c_of = iota((wide, 128), 0)
    l_of = iota((wide, 128), 1)
    k_of = c_of // 128
    lane_of = c_of % 128
    p_of = lane_of // 32
    t_of = (lane_of // 8) % 4
    fcode[...] = jnp.where((l_of == t_of * 16 + k_of) & (p_of < 3) & (t_of < 3), 1.0, 0.0).astype(
        BF16
    )

    slots = slot_ref[...]
    rolled = [slots] + [pltpu.roll(slots, 128 - 16 * a, 1) for a in range(1, 8)]
    slots = jnp.concatenate(rolled, axis=0)
    slot_hi = (slots // 128).astype(F32).astype(BF16)
    slot_lo = (slots % 128).astype(F32).astype(BF16)
    hi_all = dot(slot_hi, spread, ((1,), (0,)))
    lo_all = dot(slot_lo, spread, ((1,), (0,)))
    lane = iota((64, 128), 1)
    for k in range(16):
        cols = slice(k * 128, (k + 1) * 128)
        rows = pl.ds(k * 64, 64)
        lohot[rows, :] = jnp.where(lo_all[:, cols] == lane.astype(F32), 1.0, 0.0).astype(BF16)
        mask[rows, :] = jnp.where(hi_all[:, cols] == (lane % 8).astype(F32), 1.0, 0.0)

    dest = dest_ref[...]
    dest_hot = jnp.where(iota((64, 512), 0) == dest, 1.0, 0.0)
    dhot[...] = dest_hot.astype(BF16)
    ahead = jnp.where(iota((512, 512), 0) < iota((512, 512), 1), 1.0, 0.0).astype(BF16)
    counts = dot(dest_hot.astype(BF16), ahead, ((1,), (0,)))
    at = jnp.sum(dest_hot * counts, axis=0, keepdims=True)
    place[...] = jnp.where((iota((128, 512), 0) % 16).astype(F32) == at, 1.0, 0.0)

    voxel = voxel_ref[...]
    lo_vox[...] = jnp.where(iota((128, 512), 0) == voxel % 128, 1.0, 0.0).astype(BF16)
    over = voxel // 128
    layer_x = over // 3
    vox_row = (over - layer_x * 3) * 16 + layer_x

    sub8 = iota((8, 128), 0)
    pat = [pat_ref[0, b] for b in range(8)]
    pat_col = jnp.zeros((8, 128), I32)
    for b in range(8):
        pat_col = jnp.where(sub8 == b, pat[b], pat_col)

    def block_dot(v, table):
        high = v.astype(BF16).astype(F32)
        low = v - high
        left = jnp.concatenate([jnp.where(sub8 == b, high, 0.0) for b in range(8)], axis=1)
        right = jnp.concatenate([jnp.where(sub8 == b, low, 0.0) for b in range(8)], axis=1)
        both = jnp.concatenate([left, right], axis=0).astype(BF16)
        out = dot(both, table[...], ((1,), (0,)))
        return out[0:8, 0:128] + out[8:16, 0:128] + out[0:8, 128:256]

    def off_diagonal(v):
        partner = jnp.zeros((8, 128), F32)
        for k in range(8):
            partner = jnp.where(pat_col == k, v[k : k + 1, :], partner)
        forward = block_dot(partner, cthop)
        terms = block_dot(v, chop)
        backward = jnp.zeros((8, 128), F32)
        for b in range(8):
            backward = backward + jnp.where(sub8 == pat[b], terms[b : b + 1, :], 0.0)
        return forward + backward

    x0 = start_ref[0]
    fixed = source_ref[0] + off_diagonal(x0)
    diag = diag_ref[0]

    def collide(step):
        for z in range(2):
            for c in range(3):
                cols = slice(c * 128, (c + 1) * 128)
                f = [cur[i, z, :, cols] for i in range(19)]
                heat = [cur[19 + i, z, :, cols] for i in range(7)]
                solid = solid_ref[z, :, cols]
                rho = functools.reduce(jnp.add, f)
                m = []
                for d in range(3):
                    pos = [f[i] for i in range(19) if FLOW[i][d] == 1]
                    neg = [f[i] for i in range(19) if FLOW[i][d] == -1]
                    m.append(functools.reduce(jnp.add, pos) - functools.reduce(jnp.add, neg))
                u = [v / rho for v in m]
                flat = 1.0 - 1.5 * (u[0] * u[0] + u[1] * u[1] + u[2] * u[2])
                fluid = 1.0 - solid
                keep = fluid * (1.0 - 1.0 / TAU_FLOW)
                gain = fluid * rho * (1.0 / TAU_FLOW)
                out = [None] * 26
                out[0] = (keep + solid) * f[0] + gain * WEIGHT[0] * flat
                for i in range(1, 19, 2):
                    along = None
                    for d in range(3):
                        if FLOW[i][d] == 1:
                            along = u[d] if along is None else along + u[d]
                        elif FLOW[i][d] == -1:
                            along = -u[d] if along is None else along - u[d]
                    even = flat + 4.5 * along * along
                    odd = 3.0 * along
                    scale = gain * WEIGHT[i]
                    out[i] = keep * f[i] + solid * f[i + 1] + scale * (even + odd)
                    out[i + 1] = keep * f[i + 1] + solid * f[i] + scale * (even - odd)
                hot = functools.reduce(jnp.add, heat)
                for i in range(7):
                    share = hot * (HEAT_WEIGHT[i] / TAU_HEAT)
                    if i > 0:
                        d = [abs(v) for v in FLOW[i]].index(1)
                        sign = FLOW[i][d]
                        share = share * (1.0 + (4.0 * sign) * u[d])
                    out[19 + i] = (1.0 - 1.0 / TAU_HEAT) * heat[i] + share
                for i in range(26):
                    ez = EVERY[i][2]
                    post[i, z, :, cols] = out[i]
                    if ez == 1 and z == 1:
                        zs[step, 0, Z_UP.index(i), :, cols] = out[i]
                    if ez == -1 and z == 0:
                        zs[step, 1, Z_DOWN.index(i), :, cols] = out[i]
                    if EVERY[i][0] == 1:
                        r = X_UP.index(i) * 2 + z
                        xs[step, 0, r : r + 1, cols] = out[i][7:8, :]
                    if EVERY[i][0] == -1:
                        r = X_DOWN.index(i) * 2 + z
                        xs[step, 1, r : r + 1, cols] = out[i][0:1, :]

    def halo(step):
        made = []

        def put(n, src, dst, a, b):
            made.append(
                pltpu.make_async_remote_copy(
                    src_ref=src,
                    dst_ref=dst,
                    send_sem=halo_send.at[step, n],
                    recv_sem=halo_recv.at[step, n],
                    device_id=(a, b),
                    device_id_type=MESH,
                )
            )

        put(0, zs.at[step, 0, Z_UP.index(EDGES[0])], er.at[step, 0], g_up, s_up)
        put(1, zs.at[step, 0, Z_UP.index(EDGES[1])], er.at[step, 1], g_dn, s_up)
        put(2, zs.at[step, 1, Z_DOWN.index(EDGES[2])], er.at[step, 2], g_up, s_dn)
        put(3, zs.at[step, 1, Z_DOWN.index(EDGES[3])], er.at[step, 3], g_dn, s_dn)
        put(4, xs.at[step, 0], xr.at[step, 0], g_up, si)
        put(5, xs.at[step, 1], xr.at[step, 1], g_dn, si)
        put(6, zs.at[step, 0], zr.at[step, 0], gi, s_up)
        put(7, zs.at[step, 1], zr.at[step, 1], gi, s_dn)
        return made

    edge8 = iota((8, CY), 0)

    def stream(step):
        for i in range(26):
            ex, ey, ez = EVERY[i]
            for z in range(2):
                edge = None
                if ez == 0 or (ez == 1 and z == 1) or (ez == -1 and z == 0):
                    source = z - ez
                    piece = post[i, source]
                    if ex == 1:
                        r = X_UP.index(i) * 2 + source
                        edge = xr[step, 0, r : r + 1, :]
                    if ex == -1:
                        r = X_DOWN.index(i) * 2 + source
                        edge = xr[step, 1, r : r + 1, :]
                else:
                    if ez == 1:
                        piece = zr[step, 0, Z_UP.index(i)]
                    else:
                        piece = zr[step, 1, Z_DOWN.index(i)]
                    if ex == 1:
                        edge = er[step, EDGES.index(i), 7:8, :]
                    if ex == -1:
                        edge = er[step, EDGES.index(i), 0:1, :]
                if ex == 1:
                    piece = jnp.where(edge8 == 0, edge, pltpu.roll(piece, 1, 0))
                if ex == -1:
                    piece = jnp.where(edge8 == 7, edge, pltpu.roll(piece, 7, 0))
                if ey == 1:
                    piece = pltpu.roll(piece, 1, 1)
                if ey == -1:
                    piece = pltpu.roll(piece, CY - 1, 1)
                cur[i, z] = piece

    collide(0)
    pl.semaphore_wait(barrier, 8 + 14 + bands - 1)

    for step in range(STEPS):
        if step > 0:
            collide(step)
        made = halo(step)
        for c in made:
            c.start()
        for c in made:
            c.wait_recv()
        stream(step)

    hot_rows = []
    for z in range(2):
        hot = functools.reduce(jnp.add, [cur[19 + i, z] for i in range(7)])
        temp_out[z] = hot
        hot_rows.append(hot)
        for d in range(3):
            pos = [cur[i, z] for i in range(19) if FLOW[i][d] == 1]
            neg = [cur[i, z] for i in range(19) if FLOW[i][d] == -1]
            motion_out[d, z] = functools.reduce(jnp.add, pos) - functools.reduce(jnp.add, neg)

    table = jnp.concatenate(
        [hot_rows[z][:, c * 128 : (c + 1) * 128] for c in range(3) for z in range(2)], axis=0
    )
    picked = dot(
        jnp.concatenate(parts3(table), axis=0).astype(BF16), lo_vox[...], ((1,), (0,))
    )
    picked = picked[0:48] + picked[48:96] + picked[96:144]
    seen = jnp.sum(jnp.where(iota((48, 512), 0) == vox_row, picked, 0.0), axis=0, keepdims=True)
    coeff = coeff_ref[...]
    flux = coeff * seen
    placed = place[0:16, :]
    laid = []
    for pair in zip(parts3(flux), parts3(coeff)):
        laid.append(placed * pair[0])
        laid.append(placed * pair[1])
    laid.append(jnp.zeros((32, 512), F32))
    laid = jnp.concatenate(laid, axis=0).astype(BF16)
    sent = dot(dhot[...], laid, ((1,), (1,)))
    send1[...] = sent + pltpu.roll(sent, 96, 1) + pltpu.roll(sent, 64, 1)

    def tile(ref, n):
        return ref.at[pl.ds(pl.multiple_of(n * 8, 8), 8), :]

    def across(kind, src, dst):
        def copy(i):
            to = lax.rem(g + i, groups)
            return pltpu.make_async_remote_copy(
                src_ref=tile(src, to),
                dst_ref=tile(dst, g),
                send_sem=sems_send.at[kind, to],
                recv_sem=sems_recv.at[kind, g],
                device_id=(gi, to * 8 + j),
                device_id_type=MESH,
            )

        return copy, g, groups

    def within(kind, src, dst):
        def copy(i):
            to = lax.rem(j + i, 8)
            return pltpu.make_async_remote_copy(
                src_ref=tile(src, to),
                dst_ref=tile(dst, j),
                send_sem=sems_send.at[kind, to],
                recv_sem=sems_recv.at[kind, j],
                device_id=(gi, g * 8 + to),
                device_id_type=MESH,
            )

        return copy, j, 8

    def start_all(stage):
        copy, me, count = stage

        def go(i, carry):
            copy(i).start()
            return carry

        lax.fori_loop(1, count, go, 0)

    def finish(kind, stage, src, dst):
        copy, me, count = stage
        own = pl.ds(pl.multiple_of(me * 8, 8), 8)
        dst[own, :] = src[own, :]

        def take(i, carry):
            peer = lax.rem(me + i, count)
            pltpu.make_async_copy(
                tile(src, peer), tile(dst, peer), sems_recv.at[kind, peer]
            ).wait()
            return carry

        lax.fori_loop(1, count, take, 0)

    def turn(src, n):
        return src[pl.ds(n, 8, stride=8), :]

    stage0 = across(0, send1, recv1)
    start_all(stage0)
    finish(0, stage0, send1, recv1)
    for n in range(8):
        send2[n * 8 : (n + 1) * 8, :] = turn(recv1, n)
    stage1 = within(1, send2, recv2)
    start_all(stage1)
    finish(1, stage1, send2, recv2)

    got = recv2[...]
    in_flux = jnp.where(lane < 32, got, 0.0)
    p0, p1, p2 = parts3(in_flux)
    coded = (p0 + pltpu.roll(p1, 32, 1) + pltpu.roll(p2, 64, 1)).astype(BF16)
    values = dot(coded, ecode[...], ((1,), (0,)))
    values = jnp.concatenate([values[:, k * 128 : (k + 1) * 128] for k in range(16)], axis=0)
    values = (values * mask[...]).astype(BF16)
    summed = dot(values, lohot[...], ((0,), (0,)))
    add_source = summed[0:8] + summed[32:40] + summed[64:72]
    add_diag = summed[8:16] + summed[40:48] + summed[72:80]

    diag = diag + add_diag
    r0 = fixed + add_source - diag * x0
    w1 = (diag - SHIFT) * r0 - off_diagonal(r0)
    w2 = (diag - SHIFT) * w1 - off_diagonal(w1)
    sums = [total(r0 * r0), total(r0 * w1), total(w1 * w1), total(w1 * w2)]

    held = jnp.concatenate([x0, r0, w1, jnp.zeros((8, 128), F32)], axis=0)
    held = jnp.concatenate(list(parts3(held)) + [jnp.zeros((32, 128), F32)], axis=0).astype(BF16)
    found = dot(lohot[...], held, ((1,), (1,)))
    found = (found * mask[...]).astype(BF16)
    found = jnp.concatenate([found[k * 64 : (k + 1) * 64, :] for k in range(16)], axis=1)
    found = dot(found, fcode[...], ((1,), (0,)))
    for n in range(4):
        found = jnp.where(lane == 48 + n, sums[n], found)
    back1[...] = found

    stage2 = within(2, back1, rback1)
    start_all(stage2)
    finish(2, stage2, back1, rback1)
    lane8 = iota((8, 128), 1)
    is_sum = (lane8 >= 48) & (lane8 < 52)
    group_sum = functools.reduce(jnp.add, [rback1[n * 8 : (n + 1) * 8, :] for n in range(8)])
    for n in range(8):
        back2[n * 8 : (n + 1) * 8, :] = jnp.where(is_sum, group_sum, turn(rback1, n))
    stage3 = across(3, back2, rback2)
    start_all(stage3)
    finish(3, stage3, back2, rback2)
    tot[...] = functools.reduce(jnp.add, [rback2[n * 8 : (n + 1) * 8, :] for n in range(8)])

    def band_copy(i):
        to = lax.rem(gi + i, bands)
        return pltpu.make_async_remote_copy(
            src_ref=tot,
            dst_ref=rtot.at[gi],
            send_sem=grp_send.at[to],
            recv_sem=grp_recv.at[gi],
            device_id=(to, si),
            device_id_type=MESH,
        )

    def band_go(i, carry):
        band_copy(i).start()
        return carry

    lax.fori_loop(1, bands, band_go, 0)

    back = jnp.where(lane < 48, rback2[...], 0.0)
    rows = functools.reduce(
        jnp.add, [dot(p.astype(BF16), dhot[...], ((0,), (0,))) for p in parts3(back)]
    )
    rows = rows * place[...]
    row_x0 = jnp.sum(rows[0:16], axis=0, keepdims=True)
    row_r0 = jnp.sum(rows[16:32], axis=0, keepdims=True)
    row_w1 = jnp.sum(rows[32:48], axis=0, keepdims=True)

    rtot[gi] = tot[...]

    def band_take(i, carry):
        peer = lax.rem(gi + i, bands)
        pltpu.make_async_copy(tot, rtot.at[peer], grp_recv.at[peer]).wait()
        return carry

    lax.fori_loop(1, bands, band_take, 0)
    whole = functools.reduce(jnp.add, [rtot[n] for n in range(bands)])

    def lane_value(n):
        return total(jnp.where((lane8 == 48 + n) & (sub8 == 0), whole, 0.0))

    n0, n1, n2, n3 = [lane_value(n) for n in range(4)]
    delta = n1 / n0
    second = n2 / n0
    spread_of = second - delta * delta
    theta = SHIFT + delta
    third = n3 / n0 - 3.0 * delta * second + 2.0 * delta * delta * delta
    wide_enough = spread_of > 1e-7 * theta * theta
    spread_of = jnp.maximum(spread_of, 0.0)
    skew = jnp.where(wide_enough, third / jnp.where(wide_enough, spread_of, 1.0), 0.0)
    step0 = 1.0 / theta
    growth = spread_of / (theta * theta)
    step1 = 1.0 / (theta + skew - spread_of / theta)
    by_r0 = step0 + step1 * (growth + step0 * delta)
    by_w1 = -step1 * step0
    solid_out[0] = x0 + by_r0 * r0 + by_w1 * w1
    rows_out[...] = row_x0 + by_r0 * row_r0 + by_w1 * row_w1

    for step in range(STEPS):
        for c in halo(step):
            c.wait_send()
    for stage in (stage0, stage1, stage2, stage3):
        copy, me, count = stage

        def left(i, carry):
            copy(i).wait_send()
            return carry

        lax.fori_loop(1, count, left, 0)

    def band_left(i, carry):
        band_copy(i).wait_send()
        return carry

    lax.fori_loop(1, bands, band_left, 0)


def solution(mesh):
    bands = mesh.shape["grp"]
    subs = mesh.shape["sub"]
    groups = subs // 8

    def body(
        populations,
        heat_pops,
        solid_frac,
        coupled_grid_point,
        dest_index,
        heat_coeff,
        slot_node,
        node_diag,
        coupling,
        block_pattern,
        heat_source,
        solid_start,
    ):
        vmem = pl.BlockSpec(memory_space=pltpu.VMEM)
        smem = pl.BlockSpec(memory_space=pltpu.SMEM)
        dma = pltpu.SemaphoreType.DMA
        return pl.pallas_call(
            functools.partial(kernel, groups, bands),
            out_shape=(
                jax.ShapeDtypeStruct((2, 8, CY), F32),
                jax.ShapeDtypeStruct((3, 2, 8, CY), F32),
                jax.ShapeDtypeStruct((1, 8, 128), F32),
                jax.ShapeDtypeStruct((1, 512), F32),
            ),
            in_specs=[vmem] * 9 + [smem] + [vmem] * 2,
            out_specs=(vmem,) * 4,
            scratch_shapes=[
                pltpu.VMEM((26, 2, 8, CY), F32),
                pltpu.VMEM((26, 2, 8, CY), F32),
                pltpu.VMEM((STEPS, 2, 6, 8, CY), F32),
                pltpu.VMEM((STEPS, 2, 6, 8, CY), F32),
                pltpu.VMEM((STEPS, 2, 16, CY), F32),
                pltpu.VMEM((STEPS, 2, 16, CY), F32),
                pltpu.VMEM((STEPS, 4, 8, CY), F32),
                pltpu.VMEM((1024, 256), BF16),
                pltpu.VMEM((1024, 256), BF16),
                pltpu.VMEM((1024, 128), BF16),
                pltpu.VMEM((1024, 128), F32),
                pltpu.VMEM((128, 512), F32),
                pltpu.VMEM((64, 512), BF16),
                pltpu.VMEM((128, 512), BF16),
                pltpu.VMEM((128, 2048), BF16),
                pltpu.VMEM((2048, 128), BF16),
                *[pltpu.VMEM((64, 128), F32)] * 8,
                pltpu.VMEM((8, 128), F32),
                pltpu.VMEM((bands, 8, 128), F32),
                dma((STEPS, 8)),
                dma((STEPS, 8)),
                dma((4, 8)),
                dma((4, 8)),
                dma((bands,)),
                dma((bands,)),
            ],
            compiler_params=pltpu.CompilerParams(collective_id=0, has_side_effects=True),
            name="coupled_step",
        )(
            populations,
            heat_pops,
            solid_frac,
            coupled_grid_point,
            dest_index[..., 0],
            heat_coeff,
            slot_node.reshape(8, 128),
            node_diag,
            coupling,
            block_pattern,
            heat_source,
            solid_start,
        )

    band = P("grp", "sub")
    block = P("grp", "sub", None)
    return jax.shard_map(
        body,
        mesh=mesh,
        in_specs=(
            P(None, "sub", "grp", None),
            P(None, "sub", "grp", None),
            P("sub", "grp", None),
            band,
            block,
            band,
            band,
            block,
            P("grp", "sub", None, None),
            band,
            block,
            block,
        ),
        out_specs=(P("sub", "grp", None), P(None, "sub", "grp", None), block, band),
        check_vma=False,
    )
```

time: 351 us -> 88.7 us (0.25)
  blocking collectives: 154 us -> 0 us
  Pallas kernels: 0 us -> 83.6 us
  starting transfers between devices: 64.6 us -> 0 us
  waiting for transfers between devices: 56.4 us -> 0 us
  other arithmetic: 27.3 us -> 0 us
  local copies, waits for them, and re-layouts: 26.6 us -> 4.12 us
  matrix products: 14.5 us -> 0 us
  between operations: 7.57 us -> 0.65 us
    psum x8 -> x0, blocking collectives: 154 us -> none  [by_axis(): return functools.reduce(lax.psum, axes, shard)]
    pallas_call x0 -> x1, Pallas kernels: none -> 83.6 us  [body(): pl.pallas_call(functools.partial(kernel, groups, bands), out_shape=(jax.S...]
    all_to_all x2 -> x0, waiting for transfers between devices: 43.6 us -> none  [the longest x1 22 us: sent_together(): lax.all_to_all(both, axis, split_axis=split_dim, concat_axis=concat_dim,...]
    ppermute x8 -> x0, starting transfers between devices: 37.5 us -> none  [the longest x4 33.4 us: with_halo(): lax.ppermute(lax.slice_in_dim(block, 0, width, axis=dim), axis, backward)]
    all_to_all x2 -> x0, starting transfers between devices: 27.1 us -> none  [the longest x1 20.9 us: sent_together(): lax.all_to_all(both, axis, split_axis=split_dim, concat_axis=concat_dim,...]
    scatter-add x2 -> x0, other arithmetic: 15.5 us -> none  [body(): jnp.zeros((node_count,), jnp.float32).at[node_index]]
    dot_general x19 -> x0, matrix products: 14.5 us -> none  [the longest x3 3.56 us: flow_moments(): return jnp.tensordot(lattice, flow, axes=(0, 0), precision=highest)]
    ppermute x8 -> x0, waiting for transfers between devices: 12.9 us -> none  [the longest x4 12.1 us: with_halo(): lax.ppermute(lax.slice_in_dim(block, block.shape[dim] - width, None, axis...]
  transfers between devices with their start and end apart: 10 -> 0, of which waited for: 7 -> 0; matrix products, arithmetic and copies ran while one was open for 4% -> 0% of each run, Pallas kernels for 0% -> 0%
where the time goes in v1:
time: 88.7 us; the launch traced here: 88.4 us
  Pallas kernels  83.6 us (94%)
  local copies, waits for them, and re-layouts  4.12 us (5%)
    pallas_call x1, Pallas kernels, body(): pl.pallas_call(functools.partial(kernel, groups, bands), out_shape=(jax.S...  83.6 us
    unnamed x8, local copies, waits for them, and re-layouts  4.12 us

profile of v1, /device:TPU:1, one launch (start us, length us, event | category | flops | bytes accessed | tf_op | source)
XLA Modules:
  0.0 88.4 jit_solution(9106266206973268228)
XLA Ops:
  0.6 83.6 %coupled_step.1 = (f32[2,8,384]{2,1,0:T(8,128)}, f32[3,2,8,384]{3,2,1,0:T(8,128)}, f32[1,8,128]{2,1,0:T(8,128)}, f32[1,512]{1,0:T(1,128)}) custom-call(f32[19,2,8,384]{3,2,1,0:T(8,128)} %pops_ref.1, f32[7,2,8,384]{3,2,1,0:T(8,128)} %heat_ref.1, f32[2,8,384]{2,1,0:T(8,128)} %solid_ref.1, s32[1,512]{1,0:T(1,128)} %voxel_ref.1, s32[1,512]{1,0:T(1,128)} %bitcast.3, ...), custom_call_target="tpu_custom_call" | custom-call | tf_op jit(solution)/shard_map/coupled_step/pallas_call | solution.py:624
  84.2 1.3 %copy.20 = f32[2,8,384]{2,1,0:T(8,128)} copy(f32[2,8,384]{2,1,0:T(8,128)} %get-tuple-element.8) | data formatting | bytes 49152
  85.6 0.0 copy-start
  85.6 1.5 %copy.21 = f32[3,2,8,384]{3,2,1,0:T(8,128)} copy(f32[3,2,8,384]{3,2,1,0:T(8,128)} %get-tuple-element.9) | data formatting | bytes 147456
  87.1 0.0 copy-done
  87.1 0.0 copy-start.1
  87.1 0.6 copy.22
  87.7 0.1 copy-done.1
  87.8 0.6 copy.23
Async XLA Ops:
  85.6 1.5 %copy-start = (f32[1,8,128]{2,1,0:T(8,128)S(1)}, f32[1,8,128]{2,1,0:T(8,128)}, u32[]{:S(2)}) copy-start(f32[1,8,128]{2,1,0:T(8,128)} %get-tuple-element.10) | copy-start | bytes 12292
  87.1 0.7 copy-start.1

commit v2 on v1

--- a/solution.py
+++ b/solution.py
@@ -111,7 +111,11 @@
     lo_vox,
     ecode,
     fcode,
-    send1,
+    laid_out,
+    rel_r,
+    rel_l,
+    ring_r,
+    ring_l,
     recv1,
     send2,
     recv2,
@@ -127,6 +131,9 @@
     sems_recv,
     grp_send,
     grp_recv,
+    ready,
+    ring_send,
+    ring_recv,
 ):
     subs = groups * 8
     gi = lax.axis_index("grp")
@@ -155,75 +162,79 @@
     ):
         greet(a, b)
 
-    def greet_strip(i, carry):
-        greet(gi, lax.rem(g + i, groups) * 8 + j)
-        greet(gi, g * 8 + lax.rem(j + i, 8))
-        return carry
-
-    lax.fori_loop(1, 8, greet_strip, 0)
-
-    def greet_bands(i, carry):
-        greet(lax.rem(gi + i, bands), si)
-        return carry
-
-    lax.fori_loop(1, bands, greet_bands, 0)
-
-    cur[0:19] = pops_ref[...]
-    cur[19:26] = heat_ref[...]
+    def tell(n):
+        d = 1 << n
+        for a, b in (
+            (gi, lax.rem(si + d, subs)),
+            (gi, lax.rem(si + subs - d, subs)),
+            (lax.rem(gi + d, bands), si),
+            (lax.rem(gi + bands - d, bands), si),
+        ):
+            pl.semaphore_signal(ready.at[n], inc=1, device_id=(a, b), device_id_type=MESH)
+
+    def hear(n):
+        pl.semaphore_wait(ready.at[n], 4)
+
+    sub8 = iota((8, 128), 0)
+    lane = iota((64, 128), 1)
     xs[:, :, 8:16] = jnp.zeros((STEPS, 2, 8, CY), F32)
 
-    for b in range(8):
-        block = coup_ref[0, b]
-        high = block.astype(BF16).astype(F32)
-        low = block - high
-        rows = pl.ds(b * 128, 128)
-        chop[rows, 0:128] = high.astype(BF16)
-        chop[rows, 128:256] = low.astype(BF16)
-        cthop[rows, 0:128] = high.T.astype(BF16)
-        cthop[rows, 128:256] = low.T.astype(BF16)
-
-    wide = 16 * 128
-    a_of = iota((128, wide), 0)
-    c_of = iota((128, wide), 1)
-    k_of = c_of // 128
-    lane_of = c_of % 128
-    p_of = lane_of // 32
-    t_of = (lane_of // 8) % 4
-    ecode[...] = jnp.where(
-        (a_of == p_of * 32 + t_of * 16 + k_of) & (p_of < 3) & (t_of < 2), 1.0, 0.0
-    ).astype(BF16)
-    spread = jnp.where(a_of == k_of, 1.0, 0.0).astype(BF16)
-    c_of = iota((wide, 128), 0)
-    l_of = iota((wide, 128), 1)
-    k_of = c_of // 128
-    lane_of = c_of % 128
-    p_of = lane_of // 32
-    t_of = (lane_of // 8) % 4
-    fcode[...] = jnp.where((l_of == t_of * 16 + k_of) & (p_of < 3) & (t_of < 3), 1.0, 0.0).astype(
-        BF16
-    )
-
-    slots = slot_ref[...]
-    rolled = [slots] + [pltpu.roll(slots, 128 - 16 * a, 1) for a in range(1, 8)]
-    slots = jnp.concatenate(rolled, axis=0)
-    slot_hi = (slots // 128).astype(F32).astype(BF16)
-    slot_lo = (slots % 128).astype(F32).astype(BF16)
-    hi_all = dot(slot_hi, spread, ((1,), (0,)))
-    lo_all = dot(slot_lo, spread, ((1,), (0,)))
-    lane = iota((64, 128), 1)
-    for k in range(16):
-        cols = slice(k * 128, (k + 1) * 128)
-        rows = pl.ds(k * 64, 64)
-        lohot[rows, :] = jnp.where(lo_all[:, cols] == lane.astype(F32), 1.0, 0.0).astype(BF16)
-        mask[rows, :] = jnp.where(hi_all[:, cols] == (lane % 8).astype(F32), 1.0, 0.0)
-
-    dest = dest_ref[...]
-    dest_hot = jnp.where(iota((64, 512), 0) == dest, 1.0, 0.0)
-    dhot[...] = dest_hot.astype(BF16)
-    ahead = jnp.where(iota((512, 512), 0) < iota((512, 512), 1), 1.0, 0.0).astype(BF16)
-    counts = dot(dest_hot.astype(BF16), ahead, ((1,), (0,)))
-    at = jnp.sum(dest_hot * counts, axis=0, keepdims=True)
-    place[...] = jnp.where((iota((128, 512), 0) % 16).astype(F32) == at, 1.0, 0.0)
+    def slot_tables():
+        a_of = iota((128, 2048), 0)
+        spread = jnp.where(a_of == iota((128, 2048), 1) // 128, 1.0, 0.0).astype(BF16)
+        slots = slot_ref[...]
+        rolled = [slots] + [pltpu.roll(slots, 128 - 16 * a, 1) for a in range(1, 8)]
+        slots = jnp.concatenate(rolled, axis=0)
+        slot_hi = (slots // 128).astype(F32).astype(BF16)
+        slot_lo = (slots % 128).astype(F32).astype(BF16)
+        hi_all = dot(slot_hi, spread, ((1,), (0,)))
+        lo_all = dot(slot_lo, spread, ((1,), (0,)))
+        for k in range(16):
+            cols = slice(k * 128, (k + 1) * 128)
+            rows = pl.ds(k * 64, 64)
+            lohot[rows, :] = jnp.where(lo_all[:, cols] == lane.astype(F32), 1.0, 0.0).astype(BF16)
+            mask[rows, :] = jnp.where(hi_all[:, cols] == (lane % 8).astype(F32), 1.0, 0.0)
+
+    def row_tables():
+        dest = dest_ref[...]
+        dest_hot = jnp.where(iota((64, 512), 0) == dest, 1.0, 0.0)
+        dhot[...] = dest_hot.astype(BF16)
+        ahead = jnp.where(iota((512, 512), 0) < iota((512, 512), 1), 1.0, 0.0).astype(BF16)
+        counts = dot(dest_hot.astype(BF16), ahead, ((1,), (0,)))
+        at = jnp.sum(dest_hot * counts, axis=0, keepdims=True)
+        place[...] = jnp.where((iota((128, 512), 0) % 16).astype(F32) == at, 1.0, 0.0)
+
+    def code_tables():
+        wide = 16 * 128
+        a_of = iota((128, wide), 0)
+        c_of = iota((128, wide), 1)
+        k_of = c_of // 128
+        lane_of = c_of % 128
+        p_of = lane_of // 32
+        t_of = (lane_of // 8) % 4
+        ecode[...] = jnp.where(
+            (a_of == p_of * 32 + t_of * 16 + k_of) & (p_of < 3) & (t_of < 2), 1.0, 0.0
+        ).astype(BF16)
+        c_of = iota((wide, 128), 0)
+        l_of = iota((wide, 128), 1)
+        k_of = c_of // 128
+        lane_of = c_of % 128
+        p_of = lane_of // 32
+        t_of = (lane_of // 8) % 4
+        fcode[...] = jnp.where((l_of == t_of * 16 + k_of) & (p_of < 3) & (t_of < 3), 1.0, 0.0).astype(
+            BF16
+        )
+
+    def coupling_tables():
+        for b in range(8):
+            block = coup_ref[0, b]
+            high = block.astype(BF16).astype(F32)
+            low = block - high
+            rows = pl.ds(b * 128, 128)
+            chop[rows, 0:128] = high.astype(BF16)
+            chop[rows, 128:256] = low.astype(BF16)
+            cthop[rows, 0:128] = high.T.astype(BF16)
+            cthop[rows, 128:256] = low.T.astype(BF16)
 
     voxel = voxel_ref[...]
     lo_vox[...] = jnp.where(iota((128, 512), 0) == voxel % 128, 1.0, 0.0).astype(BF16)
@@ -231,7 +242,6 @@
     layer_x = over // 3
     vox_row = (over - layer_x * 3) * 16 + layer_x
 
-    sub8 = iota((8, 128), 0)
     pat = [pat_ref[0, b] for b in range(8)]
     pat_col = jnp.zeros((8, 128), I32)
     for b in range(8):
@@ -257,16 +267,16 @@
             backward = backward + jnp.where(sub8 == pat[b], terms[b : b + 1, :], 0.0)
         return forward + backward
 
-    x0 = start_ref[0]
-    fixed = source_ref[0] + off_diagonal(x0)
-    diag = diag_ref[0]
-
     def collide(step):
         for z in range(2):
             for c in range(3):
                 cols = slice(c * 128, (c + 1) * 128)
-                f = [cur[i, z, :, cols] for i in range(19)]
-                heat = [cur[19 + i, z, :, cols] for i in range(7)]
+                if step == 0:
+                    f = [pops_ref[i, z, :, cols] for i in range(19)]
+                    heat = [heat_ref[i, z, :, cols] for i in range(7)]
+                else:
+                    f = [cur[i, z, :, cols] for i in range(19)]
+                    heat = [cur[19 + i, z, :, cols] for i in range(7)]
                 solid = solid_ref[z, :, cols]
                 rho = functools.reduce(jnp.add, f)
                 m = []
@@ -342,11 +352,14 @@
 
     edge8 = iota((8, CY), 0)
 
-    def stream(step):
+    def stream(step, arrived):
         for i in range(26):
             ex, ey, ez = EVERY[i]
             for z in range(2):
                 edge = None
+                inside = ez == 0 or z == (1 if ez == 1 else 0)
+                if arrived == (inside and ex == 0):
+                    continue
                 if ez == 0 or (ez == 1 and z == 1) or (ez == -1 and z == 0):
                     source = z - ez
                     piece = post[i, source]
@@ -376,17 +389,36 @@
                 cur[i, z] = piece
 
     collide(0)
-    pl.semaphore_wait(barrier, 8 + 14 + bands - 1)
-
-    for step in range(STEPS):
-        if step > 0:
-            collide(step)
-        made = halo(step)
-        for c in made:
-            c.start()
-        for c in made:
-            c.wait_recv()
-        stream(step)
+    pl.semaphore_wait(barrier, 8)
+    made = halo(0)
+    for c in made:
+        c.start()
+    tell(0)
+    stream(0, False)
+    slot_tables()
+    hear(0)
+    tell(1)
+    row_tables()
+    for c in made:
+        c.wait_recv()
+    stream(0, True)
+    collide(1)
+    made = halo(1)
+    for c in made:
+        c.start()
+    hear(1)
+    tell(2)
+    stream(1, False)
+    coupling_tables()
+    code_tables()
+    x0 = start_ref[0]
+    fixed = source_ref[0] + off_diagonal(x0)
+    diag = diag_ref[0]
+
+    for c in made:
+        c.wait_recv()
+    stream(1, True)
+    hear(2)
 
     hot_rows = []
     for z in range(2):
@@ -416,7 +448,8 @@
     laid.append(jnp.zeros((32, 512), F32))
     laid = jnp.concatenate(laid, axis=0).astype(BF16)
     sent = dot(dhot[...], laid, ((1,), (1,)))
-    send1[...] = sent + pltpu.roll(sent, 96, 1) + pltpu.roll(sent, 64, 1)
+    sent = sent + pltpu.roll(sent, 96, 1) + pltpu.roll(sent, 64, 1)
+    laid_out[...] = sent
 
     def tile(ref, n):
         return ref.at[pl.ds(pl.multiple_of(n * 8, 8), 8), :]
@@ -475,9 +508,49 @@
     def turn(src, n):
         return src[pl.ds(n, 8, stride=8), :]
 
-    stage0 = across(0, send1, recv1)
-    start_all(stage0)
-    finish(0, stage0, send1, recv1)
+    def group_rows(d):
+        return pl.ds(pl.multiple_of(lax.rem(g + groups + d, groups) * 8, 8), 8)
+
+    for d in range(1, 5):
+        rel_r[(d - 1) * 8 : d * 8, :] = laid_out[group_rows(d), :]
+    for d in range(1, 4):
+        rel_l[(d - 1) * 8 : d * 8, :] = laid_out[group_rows(-d), :]
+    recv1[group_rows(0), :] = laid_out[group_rows(0), :]
+
+    def ring_copy(way, s):
+        if way == 0:
+            first, buffer, starts, most = rel_r, ring_r, (0, 32, 56, 72), 4
+            to = lax.rem(g + 1, groups)
+        else:
+            first, buffer, starts, most = rel_l, ring_l, (0, 24, 40), 3
+            to = lax.rem(g + groups - 1, groups)
+        size = (most - s) * 8
+        if s == 0:
+            src = first.at[0:size, :]
+        else:
+            src = buffer.at[starts[s - 1] + 8 : starts[s - 1] + 8 + size, :]
+        return pltpu.make_async_remote_copy(
+            src_ref=src,
+            dst_ref=buffer.at[starts[s] : starts[s] + size, :],
+            send_sem=ring_send.at[way, s],
+            recv_sem=ring_recv.at[way, s],
+            device_id=(gi, to * 8 + j),
+            device_id_type=MESH,
+        )
+
+    ring_copy(0, 0).start()
+    ring_copy(1, 0).start()
+    for s in range(4):
+        ring_copy(0, s).wait_recv()
+        if s < 3:
+            ring_copy(0, s + 1).start()
+            ring_copy(1, s).wait_recv()
+            if s < 2:
+                ring_copy(1, s + 1).start()
+            at_l = (0, 24, 40)[s]
+            recv1[group_rows(s + 1), :] = ring_l[at_l : at_l + 8, :]
+        at_r = (0, 32, 56, 72)[s]
+        recv1[group_rows(-1 - s), :] = ring_r[at_r : at_r + 8, :]
     for n in range(8):
         send2[n * 8 : (n + 1) * 8, :] = turn(recv1, n)
     stage1 = within(1, send2, recv2)
@@ -583,7 +656,9 @@
     for step in range(STEPS):
         for c in halo(step):
             c.wait_send()
-    for stage in (stage0, stage1, stage2, stage3):
+    for way, s in [(0, 0), (0, 1), (0, 2), (0, 3), (1, 0), (1, 1), (1, 2)]:
+        ring_copy(way, s).wait_send()
+    for stage in (stage1, stage2, stage3):
         copy, me, count = stage
 
         def left(i, carry):
@@ -597,6 +672,11 @@
         return carry
 
     lax.fori_loop(1, bands, band_left, 0)
+
+
+def publish(*refs):
+    for source, target in zip(refs[:4], refs[4:]):
+        target[...] = source[...]
 
 
 def solution(mesh):
@@ -621,14 +701,15 @@
         vmem = pl.BlockSpec(memory_space=pltpu.VMEM)
         smem = pl.BlockSpec(memory_space=pltpu.SMEM)
         dma = pltpu.SemaphoreType.DMA
-        return pl.pallas_call(
-            functools.partial(kernel, groups, bands),
-            out_shape=(
+        shapes = (
                 jax.ShapeDtypeStruct((2, 8, CY), F32),
                 jax.ShapeDtypeStruct((3, 2, 8, CY), F32),
                 jax.ShapeDtypeStruct((1, 8, 128), F32),
                 jax.ShapeDtypeStruct((1, 512), F32),
-            ),
+            )
+        made = pl.pallas_call(
+            functools.partial(kernel, groups, bands),
+            out_shape=shapes,
             in_specs=[vmem] * 9 + [smem] + [vmem] * 2,
             out_specs=(vmem,) * 4,
             scratch_shapes=[
@@ -648,7 +729,12 @@
                 pltpu.VMEM((128, 512), BF16),
                 pltpu.VMEM((128, 2048), BF16),
                 pltpu.VMEM((2048, 128), BF16),
-                *[pltpu.VMEM((64, 128), F32)] * 8,
+                pltpu.VMEM((64, 128), F32),
+                pltpu.VMEM((32, 128), F32),
+                pltpu.VMEM((24, 128), F32),
+                pltpu.VMEM((80, 128), F32),
+                pltpu.VMEM((48, 128), F32),
+                *[pltpu.VMEM((64, 128), F32)] * 7,
                 pltpu.VMEM((8, 128), F32),
                 pltpu.VMEM((bands, 8, 128), F32),
                 dma((STEPS, 8)),
@@ -657,6 +743,9 @@
                 dma((4, 8)),
                 dma((bands,)),
                 dma((bands,)),
+                pltpu.SemaphoreType.REGULAR((3,)),
+                dma((2, 4)),
+                dma((2, 4)),
             ],
             compiler_params=pltpu.CompilerParams(collective_id=0, has_side_effects=True),
             name="coupled_step",
@@ -674,6 +763,13 @@
             heat_source,
             solid_start,
         )
+        return pl.pallas_call(
+            publish,
+            out_shape=shapes,
+            in_specs=[vmem] * 4,
+            out_specs=(vmem,) * 4,
+            name="publish",
+        )(*made)
 
     band = P("grp", "sub")
     block = P("grp", "sub", None)

time: 88.7 us -> 81 us (0.913)
  local copies, waits for them, and re-layouts: 4.12 us -> 0 us
  Pallas kernels: 83.6 us -> 80.2 us
    unnamed x8 -> x0, local copies, waits for them, and re-layouts: 4.12 us -> none
    pallas_call x1 -> x2, Pallas kernels: 83.6 us -> 80.2 us  [the longest x1 78.7 us: body(): pl.pallas_call(functools.partial(kernel, groups, bands), out_shape=shapes...]
where the time goes in v2:
time: 81 us; the launch traced here: 80.8 us
  Pallas kernels  80.2 us (99%)
    pallas_call x1, Pallas kernels, body(): pl.pallas_call(functools.partial(kernel, groups, bands), out_shape=shapes...  78.7 us

profile of v2, /device:TPU:1, one launch (start us, length us, event | category | flops | bytes accessed | tf_op | source)
XLA Modules:
  0.0 80.8 jit_solution(11957512572614094894)
XLA Ops:
  0.6 78.7 %coupled_step.1 = (f32[2,8,384]{2,1,0:T(8,128)}, f32[3,2,8,384]{3,2,1,0:T(8,128)}, f32[1,8,128]{2,1,0:T(8,128)}, f32[1,512]{1,0:T(1,128)}) custom-call(f32[19,2,8,384]{3,2,1,0:T(8,128)} %pops_ref.1, f32[7,2,8,384]{3,2,1,0:T(8,128)} %heat_ref.1, f32[2,8,384]{2,1,0:T(8,128)} %solid_ref.1, s32[1,512]{1,0:T(1,128)} %voxel_ref.1, s32[1,512]{1,0:T(1,128)} %bitcast.3, ...), custom_call_target="tpu_custom_call" | custom-call | tf_op jit(solution)/shard_map/coupled_step/pallas_call | solution.py:710
  79.3 1.5 %publish.1 = (f32[2,8,384]{2,1,0:T(8,128)}, f32[3,2,8,384]{3,2,1,0:T(8,128)}, f32[1,8,128]{2,1,0:T(8,128)}, f32[1,512]{1,0:T(1,128)}) custom-call(f32[2,8,384]{2,1,0:T(8,128)} %get-tuple-element.8.refs_0_, f32[3,2,8,384]{3,2,1,0:T(8,128)} %get-tuple-element.9.refs_1_, f32[1,8,128]{2,1,0:T(8,128)} %get-tuple-element.10.refs_2_, ...), custom_call_target="tpu_custom_call" | custom-call | tf_op jit(solution)/shard_map/publish/pallas_call | solution.py:766

commit v3 on v2

--- a/solution.py
+++ b/solution.py
@@ -112,28 +112,18 @@
     ecode,
     fcode,
     laid_out,
-    rel_r,
-    rel_l,
-    ring_r,
-    ring_l,
-    recv1,
-    send2,
-    recv2,
-    back1,
-    rback1,
-    back2,
-    rback2,
+    landed,
+    returned,
+    received,
     tot,
     rtot,
     halo_send,
     halo_recv,
-    sems_send,
-    sems_recv,
-    grp_send,
-    grp_recv,
+    strip_send,
+    strip_recv,
+    band_send,
+    band_recv,
     ready,
-    ring_send,
-    ring_recv,
 ):
     subs = groups * 8
     gi = lax.axis_index("grp")
@@ -164,16 +154,14 @@
 
     def tell(n):
         d = 1 << n
-        for a, b in (
-            (gi, lax.rem(si + d, subs)),
-            (gi, lax.rem(si + subs - d, subs)),
-            (lax.rem(gi + d, bands), si),
-            (lax.rem(gi + bands - d, bands), si),
-        ):
+        to = [(gi, lax.rem(si + d, subs)), (gi, lax.rem(si + subs - d, subs))]
+        if 2 * d < bands:
+            to += [(lax.rem(gi + d, bands), si), (lax.rem(gi + bands - d, bands), si)]
+        for a, b in to:
             pl.semaphore_signal(ready.at[n], inc=1, device_id=(a, b), device_id_type=MESH)
 
     def hear(n):
-        pl.semaphore_wait(ready.at[n], 4)
+        pl.semaphore_wait(ready.at[n], 4 if 2 << n < bands else 2)
 
     sub8 = iota((8, 128), 0)
     lane = iota((64, 128), 1)
@@ -399,6 +387,12 @@
     hear(0)
     tell(1)
     row_tables()
+    hear(1)
+    tell(2)
+    coupling_tables()
+    hear(2)
+    tell(3)
+    code_tables()
     for c in made:
         c.wait_recv()
     stream(0, True)
@@ -406,19 +400,15 @@
     made = halo(1)
     for c in made:
         c.start()
-    hear(1)
-    tell(2)
+    hear(3)
+    tell(4)
     stream(1, False)
-    coupling_tables()
-    code_tables()
     x0 = start_ref[0]
     fixed = source_ref[0] + off_diagonal(x0)
     diag = diag_ref[0]
-
     for c in made:
         c.wait_recv()
     stream(1, True)
-    hear(2)
 
     hot_rows = []
     for z in range(2):
@@ -449,115 +439,42 @@
     laid = jnp.concatenate(laid, axis=0).astype(BF16)
     sent = dot(dhot[...], laid, ((1,), (1,)))
     sent = sent + pltpu.roll(sent, 96, 1) + pltpu.roll(sent, 64, 1)
-    laid_out[...] = sent
-
-    def tile(ref, n):
-        return ref.at[pl.ds(pl.multiple_of(n * 8, 8), 8), :]
-
-    def across(kind, src, dst):
-        def copy(i):
-            to = lax.rem(g + i, groups)
-            return pltpu.make_async_remote_copy(
-                src_ref=tile(src, to),
-                dst_ref=tile(dst, g),
-                send_sem=sems_send.at[kind, to],
-                recv_sem=sems_recv.at[kind, g],
-                device_id=(gi, to * 8 + j),
-                device_id_type=MESH,
-            )
-
-        return copy, g, groups
-
-    def within(kind, src, dst):
-        def copy(i):
-            to = lax.rem(j + i, 8)
-            return pltpu.make_async_remote_copy(
-                src_ref=tile(src, to),
-                dst_ref=tile(dst, j),
-                send_sem=sems_send.at[kind, to],
-                recv_sem=sems_recv.at[kind, j],
-                device_id=(gi, g * 8 + to),
-                device_id_type=MESH,
-            )
-
-        return copy, j, 8
-
-    def start_all(stage):
-        copy, me, count = stage
-
-        def go(i, carry):
-            copy(i).start()
-            return carry
-
-        lax.fori_loop(1, count, go, 0)
-
-    def finish(kind, stage, src, dst):
-        copy, me, count = stage
-        own = pl.ds(pl.multiple_of(me * 8, 8), 8)
-        dst[own, :] = src[own, :]
-
-        def take(i, carry):
-            peer = lax.rem(me + i, count)
-            pltpu.make_async_copy(
-                tile(src, peer), tile(dst, peer), sems_recv.at[kind, peer]
-            ).wait()
-            return carry
-
-        lax.fori_loop(1, count, take, 0)
-
-    def turn(src, n):
-        return src[pl.ds(n, 8, stride=8), :]
-
-    def group_rows(d):
-        return pl.ds(pl.multiple_of(lax.rem(g + groups + d, groups) * 8, 8), 8)
-
-    for d in range(1, 5):
-        rel_r[(d - 1) * 8 : d * 8, :] = laid_out[group_rows(d), :]
-    for d in range(1, 4):
-        rel_l[(d - 1) * 8 : d * 8, :] = laid_out[group_rows(-d), :]
-    recv1[group_rows(0), :] = laid_out[group_rows(0), :]
-
-    def ring_copy(way, s):
+    laid_out[...] = sent.reshape(64, 1, 128)
+
+    def strip_copy(way, i):
+        d = subs // 2 + (1 - 2 * (i % 2)) * ((i + 1) // 2)
+        to = lax.rem(si + d, subs)
         if way == 0:
-            first, buffer, starts, most = rel_r, ring_r, (0, 32, 56, 72), 4
-            to = lax.rem(g + 1, groups)
+            src, dst = laid_out.at[to], landed.at[j * groups + g]
         else:
-            first, buffer, starts, most = rel_l, ring_l, (0, 24, 40), 3
-            to = lax.rem(g + groups - 1, groups)
-        size = (most - s) * 8
-        if s == 0:
-            src = first.at[0:size, :]
-        else:
-            src = buffer.at[starts[s - 1] + 8 : starts[s - 1] + 8 + size, :]
+            src, dst = returned.at[(to % 8) * groups + to // 8], received.at[si]
         return pltpu.make_async_remote_copy(
             src_ref=src,
-            dst_ref=buffer.at[starts[s] : starts[s] + size, :],
-            send_sem=ring_send.at[way, s],
-            recv_sem=ring_recv.at[way, s],
-            device_id=(gi, to * 8 + j),
+            dst_ref=dst,
+            send_sem=strip_send.at[way],
+            recv_sem=strip_recv.at[way],
+            device_id=(gi, to),
             device_id_type=MESH,
         )
 
-    ring_copy(0, 0).start()
-    ring_copy(1, 0).start()
-    for s in range(4):
-        ring_copy(0, s).wait_recv()
-        if s < 3:
-            ring_copy(0, s + 1).start()
-            ring_copy(1, s).wait_recv()
-            if s < 2:
-                ring_copy(1, s + 1).start()
-            at_l = (0, 24, 40)[s]
-            recv1[group_rows(s + 1), :] = ring_l[at_l : at_l + 8, :]
-        at_r = (0, 32, 56, 72)[s]
-        recv1[group_rows(-1 - s), :] = ring_r[at_r : at_r + 8, :]
-    for n in range(8):
-        send2[n * 8 : (n + 1) * 8, :] = turn(recv1, n)
-    stage1 = within(1, send2, recv2)
-    start_all(stage1)
-    finish(1, stage1, send2, recv2)
-
-    got = recv2[...]
+    def strip_start(way):
+        def go(i, carry):
+            strip_copy(way, i).start()
+            return carry
+
+        lax.fori_loop(0, subs - 1, go, 0)
+
+    def strip_all(way, sem):
+        src, dst = (laid_out, landed) if way == 0 else (returned, received)
+        rest = pl.ds(0, subs - 1)
+        return pltpu.make_async_copy(src.at[rest], dst.at[rest], sem.at[way])
+
+    hear(4)
+    strip_start(0)
+    landed[j * groups + g] = laid_out[si]
+    strip_all(0, strip_recv).wait()
+
+    got = landed[...].reshape(64, 128)
     in_flux = jnp.where(lane < 32, got, 0.0)
     p0, p1, p2 = parts3(in_flux)
     coded = (p0 + pltpu.roll(p1, 32, 1) + pltpu.roll(p2, 64, 1)).astype(BF16)
@@ -582,29 +499,20 @@
     found = dot(found, fcode[...], ((1,), (0,)))
     for n in range(4):
         found = jnp.where(lane == 48 + n, sums[n], found)
-    back1[...] = found
-
-    stage2 = within(2, back1, rback1)
-    start_all(stage2)
-    finish(2, stage2, back1, rback1)
-    lane8 = iota((8, 128), 1)
-    is_sum = (lane8 >= 48) & (lane8 < 52)
-    group_sum = functools.reduce(jnp.add, [rback1[n * 8 : (n + 1) * 8, :] for n in range(8)])
-    for n in range(8):
-        back2[n * 8 : (n + 1) * 8, :] = jnp.where(is_sum, group_sum, turn(rback1, n))
-    stage3 = across(3, back2, rback2)
-    start_all(stage3)
-    finish(3, stage3, back2, rback2)
-    tot[...] = functools.reduce(jnp.add, [rback2[n * 8 : (n + 1) * 8, :] for n in range(8)])
+    returned[...] = found.reshape(64, 1, 128)
+    strip_start(1)
+    received[si] = returned[j * groups + g]
+    strip_all(1, strip_recv).wait()
+    back = received[...].reshape(64, 128)
+    tot[...] = jnp.sum(back, axis=0, keepdims=True)
 
     def band_copy(i):
-        to = lax.rem(gi + i, bands)
         return pltpu.make_async_remote_copy(
             src_ref=tot,
             dst_ref=rtot.at[gi],
-            send_sem=grp_send.at[to],
-            recv_sem=grp_recv.at[gi],
-            device_id=(to, si),
+            send_sem=band_send,
+            recv_sem=band_recv,
+            device_id=(lax.rem(gi + i, bands), si),
             device_id_type=MESH,
         )
 
@@ -614,7 +522,11 @@
 
     lax.fori_loop(1, bands, band_go, 0)
 
-    back = jnp.where(lane < 48, rback2[...], 0.0)
+    def band_all(sem):
+        rest = pl.ds(0, bands - 1)
+        return pltpu.make_async_copy(laid_out.at[rest], rtot.at[rest], sem)
+
+    back = jnp.where(lane < 48, back, 0.0)
     rows = functools.reduce(
         jnp.add, [dot(p.astype(BF16), dhot[...], ((0,), (0,))) for p in parts3(back)]
     )
@@ -625,16 +537,12 @@
 
     rtot[gi] = tot[...]
 
-    def band_take(i, carry):
-        peer = lax.rem(gi + i, bands)
-        pltpu.make_async_copy(tot, rtot.at[peer], grp_recv.at[peer]).wait()
-        return carry
-
-    lax.fori_loop(1, bands, band_take, 0)
+    band_all(band_recv).wait()
+    lane1 = iota((1, 128), 1)
     whole = functools.reduce(jnp.add, [rtot[n] for n in range(bands)])
 
     def lane_value(n):
-        return total(jnp.where((lane8 == 48 + n) & (sub8 == 0), whole, 0.0))
+        return jnp.sum(jnp.where(lane1 == 48 + n, whole, 0.0), axis=1, keepdims=True)
 
     n0, n1, n2, n3 = [lane_value(n) for n in range(4)]
     delta = n1 / n0
@@ -656,22 +564,9 @@
     for step in range(STEPS):
         for c in halo(step):
             c.wait_send()
-    for way, s in [(0, 0), (0, 1), (0, 2), (0, 3), (1, 0), (1, 1), (1, 2)]:
-        ring_copy(way, s).wait_send()
-    for stage in (stage1, stage2, stage3):
-        copy, me, count = stage
-
-        def left(i, carry):
-            copy(i).wait_send()
-            return carry
-
-        lax.fori_loop(1, count, left, 0)
-
-    def band_left(i, carry):
-        band_copy(i).wait_send()
-        return carry
-
-    lax.fori_loop(1, bands, band_left, 0)
+    strip_all(0, strip_send).wait()
+    strip_all(1, strip_send).wait()
+    band_all(band_send).wait()
 
 
 def publish(*refs):
@@ -729,23 +624,16 @@
                 pltpu.VMEM((128, 512), BF16),
                 pltpu.VMEM((128, 2048), BF16),
                 pltpu.VMEM((2048, 128), BF16),
-                pltpu.VMEM((64, 128), F32),
-                pltpu.VMEM((32, 128), F32),
-                pltpu.VMEM((24, 128), F32),
-                pltpu.VMEM((80, 128), F32),
-                pltpu.VMEM((48, 128), F32),
-                *[pltpu.VMEM((64, 128), F32)] * 7,
-                pltpu.VMEM((8, 128), F32),
-                pltpu.VMEM((bands, 8, 128), F32),
+                *[pltpu.VMEM((64, 1, 128), F32)] * 4,
+                pltpu.VMEM((1, 128), F32),
+                pltpu.VMEM((bands, 1, 128), F32),
                 dma((STEPS, 8)),
                 dma((STEPS, 8)),
-                dma((4, 8)),
-                dma((4, 8)),
-                dma((bands,)),
-                dma((bands,)),
-                pltpu.SemaphoreType.REGULAR((3,)),
-                dma((2, 4)),
-                dma((2, 4)),
+                dma((2,)),
+                dma((2,)),
+                dma,
+                dma,
+                pltpu.SemaphoreType.REGULAR((5,)),
             ],
             compiler_params=pltpu.CompilerParams(collective_id=0, has_side_effects=True),
             name="coupled_step",

time: 81 us -> 71.9 us (0.89)
  Pallas kernels: 80.2 us -> 71 us
    pallas_call x1, Pallas kernels: 78.7 us -> 69.5 us  [body(): pl.pallas_call(functools.partial(kernel, groups, bands), out_shape=shapes...]
where the time goes in v3:
time: 71.9 us; the launch traced here: 71.7 us
  Pallas kernels  71 us (99%)
    pallas_call x1, Pallas kernels, body(): pl.pallas_call(functools.partial(kernel, groups, bands), out_shape=shapes...  69.5 us
    pallas_call x1, Pallas kernels, body(): pl.pallas_call(publish, out_shape=shapes, in_specs=[vmem] * 4, out_specs=...  1.53 us

profile of v3, /device:TPU:1, one launch (start us, length us, event | category | flops | bytes accessed | tf_op | source)
XLA Modules:
  0.0 71.7 jit_solution(13468725727021408573)
XLA Ops:
  0.6 69.5 %coupled_step.1 = (f32[2,8,384]{2,1,0:T(8,128)}, f32[3,2,8,384]{3,2,1,0:T(8,128)}, f32[1,8,128]{2,1,0:T(8,128)}, f32[1,512]{1,0:T(1,128)}) custom-call(f32[19,2,8,384]{3,2,1,0:T(8,128)} %pops_ref.1, f32[7,2,8,384]{3,2,1,0:T(8,128)} %heat_ref.1, f32[2,8,384]{2,1,0:T(8,128)} %solid_ref.1, s32[1,512]{1,0:T(1,128)} %voxel_ref.1, s32[1,512]{1,0:T(1,128)} %bitcast.3, ...), custom_call_target="tpu_custom_call" | custom-call | tf_op jit(solution)/shard_map/coupled_step/pallas_call | solution.py:605
  70.2 1.5 %publish.1 = (f32[2,8,384]{2,1,0:T(8,128)}, f32[3,2,8,384]{3,2,1,0:T(8,128)}, f32[1,8,128]{2,1,0:T(8,128)}, f32[1,512]{1,0:T(1,128)}) custom-call(f32[2,8,384]{2,1,0:T(8,128)} %get-tuple-element.8.refs_0_, f32[3,2,8,384]{3,2,1,0:T(8,128)} %get-tuple-element.9.refs_1_, f32[1,8,128]{2,1,0:T(8,128)} %get-tuple-element.10.refs_2_, ...), custom_call_target="tpu_custom_call" | custom-call | tf_op jit(solution)/shard_map/publish/pallas_call | solution.py:654

commit v4 on v3

--- a/solution.py
+++ b/solution.py
@@ -112,6 +112,8 @@
     ecode,
     fcode,
     laid_out,
+    block_out,
+    block_in,
     landed,
     returned,
     received,
@@ -123,6 +125,8 @@
     strip_recv,
     band_send,
     band_recv,
+    block_send,
+    block_recv,
     ready,
 ):
     subs = groups * 8
@@ -400,8 +404,6 @@
     made = halo(1)
     for c in made:
         c.start()
-    hear(3)
-    tell(4)
     stream(1, False)
     x0 = start_ref[0]
     fixed = source_ref[0] + off_diagonal(x0)
@@ -441,37 +443,90 @@
     sent = sent + pltpu.roll(sent, 96, 1) + pltpu.roll(sent, 64, 1)
     laid_out[...] = sent.reshape(64, 1, 128)
 
-    def strip_copy(way, i):
-        d = subs // 2 + (1 - 2 * (i % 2)) * ((i + 1) // 2)
-        to = lax.rem(si + d, subs)
-        if way == 0:
-            src, dst = laid_out.at[to], landed.at[j * groups + g]
-        else:
-            src, dst = returned.at[(to % 8) * groups + to // 8], received.at[si]
+    half = subs // 4
+
+    def landing(source):
+        return landed.at[(source % 8) * groups + source // 8]
+
+    def row_copy(src, source, to):
         return pltpu.make_async_remote_copy(
             src_ref=src,
-            dst_ref=dst,
-            send_sem=strip_send.at[way],
-            recv_sem=strip_recv.at[way],
+            dst_ref=landing(source),
+            send_sem=strip_send.at[0],
+            recv_sem=strip_recv.at[0],
             device_id=(gi, to),
             device_id_type=MESH,
         )
 
-    def strip_start(way):
-        def go(i, carry):
-            strip_copy(way, i).start()
+    for e in range(1, half + 1):
+        block_out[0, e - 1] = laid_out[lax.rem(si + half + e, subs)]
+        block_out[1, e - 1] = laid_out[lax.rem(si + subs - half - e, subs)]
+
+    def block_copy(way):
+        to = lax.rem(si + (half if way == 0 else subs - half), subs)
+        return pltpu.make_async_remote_copy(
+            src_ref=block_out.at[way],
+            dst_ref=block_in.at[way],
+            send_sem=block_send.at[way],
+            recv_sem=block_recv.at[way],
+            device_id=(gi, to),
+            device_id_type=MESH,
+        )
+
+    hear(3)
+    block_copy(0).start()
+    block_copy(1).start()
+
+    def near(i, carry):
+        d = (half - i // 2) * (1 - 2 * (i % 2))
+        to = lax.rem(si + subs + d, subs)
+        row_copy(laid_out.at[to], si, to).start()
+        return carry
+
+    lax.fori_loop(0, 2 * half, near, 0)
+    landed[j * groups + g] = laid_out[si]
+
+    early = si // (subs // 2)
+    for way in (early, 1 - early):
+        pltpu.make_async_copy(block_out.at[way], block_in.at[way], block_recv.at[way]).wait()
+        sign = 1 - 2 * way
+        source = lax.rem(si + subs - sign * half, subs)
+
+        def forward(e, way=way, sign=sign, source=source):
+            to = lax.rem(si + subs + sign * e, subs)
+            row_copy(block_in.at[way, e - 1], source, to).start()
+
+        @pl.when(way == 0)
+        def _(forward=forward):
+            forward(half)
+
+        def forward_all(i, carry, forward=forward):
+            forward(half - 1 - i)
             return carry
 
-        lax.fori_loop(0, subs - 1, go, 0)
+        lax.fori_loop(0, half - 1, forward_all, 0)
+
+    def back_copy(i):
+        d = subs // 2 + (1 - 2 * (i % 2)) * ((i + 1) // 2)
+        to = lax.rem(si + d, subs)
+        return pltpu.make_async_remote_copy(
+            src_ref=returned.at[(to % 8) * groups + to // 8],
+            dst_ref=received.at[si],
+            send_sem=strip_send.at[1],
+            recv_sem=strip_recv.at[1],
+            device_id=(gi, to),
+            device_id_type=MESH,
+        )
+
+    def back_go(i, carry):
+        back_copy(i).start()
+        return carry
 
     def strip_all(way, sem):
         src, dst = (laid_out, landed) if way == 0 else (returned, received)
         rest = pl.ds(0, subs - 1)
         return pltpu.make_async_copy(src.at[rest], dst.at[rest], sem.at[way])
 
-    hear(4)
-    strip_start(0)
-    landed[j * groups + g] = laid_out[si]
     strip_all(0, strip_recv).wait()
 
     got = landed[...].reshape(64, 128)
@@ -500,7 +555,7 @@
     for n in range(4):
         found = jnp.where(lane == 48 + n, sums[n], found)
     returned[...] = found.reshape(64, 1, 128)
-    strip_start(1)
+    lax.fori_loop(0, subs - 1, back_go, 0)
     received[si] = returned[j * groups + g]
     strip_all(1, strip_recv).wait()
     back = received[...].reshape(64, 128)
@@ -564,6 +619,8 @@
     for step in range(STEPS):
         for c in halo(step):
             c.wait_send()
+    block_copy(0).wait_send()
+    block_copy(1).wait_send()
     strip_all(0, strip_send).wait()
     strip_all(1, strip_send).wait()
     band_all(band_send).wait()
@@ -604,7 +661,7 @@
             )
         made = pl.pallas_call(
             functools.partial(kernel, groups, bands),
-            out_shape=shapes,
+            out_shape=tuple(pltpu.VMEM(v.shape, v.dtype) for v in shapes),
             in_specs=[vmem] * 9 + [smem] + [vmem] * 2,
             out_specs=(vmem,) * 4,
             scratch_shapes=[
@@ -624,7 +681,9 @@
                 pltpu.VMEM((128, 512), BF16),
                 pltpu.VMEM((128, 2048), BF16),
                 pltpu.VMEM((2048, 128), BF16),
-                *[pltpu.VMEM((64, 1, 128), F32)] * 4,
+                pltpu.VMEM((64, 1, 128), F32),
+                *[pltpu.VMEM((2, 16, 1, 128), F32)] * 2,
+                *[pltpu.VMEM((64, 1, 128), F32)] * 3,
                 pltpu.VMEM((1, 128), F32),
                 pltpu.VMEM((bands, 1, 128), F32),
                 dma((STEPS, 8)),
@@ -633,7 +692,9 @@
                 dma((2,)),
                 dma,
                 dma,
-                pltpu.SemaphoreType.REGULAR((5,)),
+                dma((2,)),
+                dma((2,)),
+                pltpu.SemaphoreType.REGULAR((4,)),
             ],
             compiler_params=pltpu.CompilerParams(collective_id=0, has_side_effects=True),
             name="coupled_step",
@@ -657,7 +718,7 @@
             in_specs=[vmem] * 4,
             out_specs=(vmem,) * 4,
             name="publish",
-        )(*made)
+        )(*[pltpu.with_memory_space_constraint(v, pltpu.VMEM) for v in made])
 
     band = P("grp", "sub")
     block = P("grp", "sub", None)

time: 71.9 us -> 67.9 us (0.944)
  Pallas kernels: 71 us -> 67.1 us
    pallas_call x1, Pallas kernels: 69.5 us -> 66.5 us  [body(): pl.pallas_call(functools.partial(kernel, groups, bands), out_shape=tuple(...]
    pallas_call x1, Pallas kernels: 1.53 us -> 0.65 us  [body(): pl.pallas_call(publish, out_shape=shapes, in_specs=[vmem] * 4, out_specs=...]
where the time goes in v4:
time: 67.9 us; the launch traced here: 67.7 us
  Pallas kernels  67.1 us (99%)
    pallas_call x1, Pallas kernels, body(): pl.pallas_call(functools.partial(kernel, groups, bands), out_shape=tuple(...  66.5 us

profile of v4, /device:TPU:1, one launch (start us, length us, event | category | flops | bytes accessed | tf_op | source)
XLA Modules:
  0.0 67.7 jit_solution(2655489474901264584)
XLA Ops:
  0.6 66.5 %coupled_step.1 = (f32[2,8,384]{2,1,0:T(8,128)S(1)}, f32[3,2,8,384]{3,2,1,0:T(8,128)S(1)}, f32[1,8,128]{2,1,0:T(8,128)S(1)}, f32[1,512]{1,0:T(1,128)S(1)}) custom-call(f32[19,2,8,384]{3,2,1,0:T(8,128)} %pops_ref.1, f32[7,2,8,384]{3,2,1,0:T(8,128)} %heat_ref.1, f32[2,8,384]{2,1,0:T(8,128)} %solid_ref.1, s32[1,512]{1,0:T(1,128)} %voxel_ref.1, ...), custom_call_target="tpu_custom_call" | custom-call | tf_op jit(solution)/shard_map/coupled_step/pallas_call | solution.py:662
  67.1 0.6 publish.1

commit v5 on v4

--- a/solution.py
+++ b/solution.py
@@ -105,6 +105,11 @@
     chop,
     cthop,
     lohot,
+    lohot_t,
+    xh_s,
+    xh_r,
+    vel,
+    coup,
     mask,
     place,
     dhot,
@@ -127,6 +132,9 @@
     band_recv,
     block_send,
     block_recv,
+    heat_send,
+    heat_recv,
+    coup_sem,
     ready,
 ):
     subs = groups * 8
@@ -139,6 +147,8 @@
     s_up = lax.rem(si + 1, subs)
     s_dn = lax.rem(si + subs - 1, subs)
 
+    fetch = pltpu.make_async_copy(coup_ref.at[0], coup, coup_sem)
+    fetch.start()
     barrier = pltpu.get_barrier_semaphore()
 
     def greet(a, b):
@@ -170,6 +180,7 @@
     sub8 = iota((8, 128), 0)
     lane = iota((64, 128), 1)
     xs[:, :, 8:16] = jnp.zeros((STEPS, 2, 8, CY), F32)
+    xh_s[...] = jnp.zeros((2, 8, CY), F32)
 
     def slot_tables():
         a_of = iota((128, 2048), 0)
@@ -185,6 +196,9 @@
             cols = slice(k * 128, (k + 1) * 128)
             rows = pl.ds(k * 64, 64)
             lohot[rows, :] = jnp.where(lo_all[:, cols] == lane.astype(F32), 1.0, 0.0).astype(BF16)
+            lohot_t[:, k * 64 : (k + 1) * 64] = (
+                jnp.where(lo_all[:, cols] == lane.astype(F32), 1.0, 0.0).T.astype(BF16)
+            )
             mask[rows, :] = jnp.where(hi_all[:, cols] == (lane % 8).astype(F32), 1.0, 0.0)
 
     def row_tables():
@@ -219,7 +233,7 @@
 
     def coupling_tables():
         for b in range(8):
-            block = coup_ref[0, b]
+            block = coup[b]
             high = block.astype(BF16).astype(F32)
             low = block - high
             rows = pl.ds(b * 128, 128)
@@ -259,7 +273,7 @@
             backward = backward + jnp.where(sub8 == pat[b], terms[b : b + 1, :], 0.0)
         return forward + backward
 
-    def collide(step):
+    def collide(step, part):
         for z in range(2):
             for c in range(3):
                 cols = slice(c * 128, (c + 1) * 128)
@@ -269,53 +283,68 @@
                 else:
                     f = [cur[i, z, :, cols] for i in range(19)]
                     heat = [cur[19 + i, z, :, cols] for i in range(7)]
-                solid = solid_ref[z, :, cols]
-                rho = functools.reduce(jnp.add, f)
-                m = []
-                for d in range(3):
-                    pos = [f[i] for i in range(19) if FLOW[i][d] == 1]
-                    neg = [f[i] for i in range(19) if FLOW[i][d] == -1]
-                    m.append(functools.reduce(jnp.add, pos) - functools.reduce(jnp.add, neg))
-                u = [v / rho for v in m]
-                flat = 1.0 - 1.5 * (u[0] * u[0] + u[1] * u[1] + u[2] * u[2])
-                fluid = 1.0 - solid
-                keep = fluid * (1.0 - 1.0 / TAU_FLOW)
-                gain = fluid * rho * (1.0 / TAU_FLOW)
+                if part == "flow":
+                    rho = vel[3, z, :, cols]
+                    u = [vel[d, z, :, cols] for d in range(3)]
+                else:
+                    rho = functools.reduce(jnp.add, f)
+                    m = []
+                    for d in range(3):
+                        pos = [f[i] for i in range(19) if FLOW[i][d] == 1]
+                        neg = [f[i] for i in range(19) if FLOW[i][d] == -1]
+                        m.append(functools.reduce(jnp.add, pos) - functools.reduce(jnp.add, neg))
+                    u = [v / rho for v in m]
+                if part == "heat":
+                    vel[3, z, :, cols] = rho
+                    for d in range(3):
+                        vel[d, z, :, cols] = u[d]
                 out = [None] * 26
-                out[0] = (keep + solid) * f[0] + gain * WEIGHT[0] * flat
-                for i in range(1, 19, 2):
-                    along = None
-                    for d in range(3):
-                        if FLOW[i][d] == 1:
-                            along = u[d] if along is None else along + u[d]
-                        elif FLOW[i][d] == -1:
-                            along = -u[d] if along is None else along - u[d]
-                    even = flat + 4.5 * along * along
-                    odd = 3.0 * along
-                    scale = gain * WEIGHT[i]
-                    out[i] = keep * f[i] + solid * f[i + 1] + scale * (even + odd)
-                    out[i + 1] = keep * f[i + 1] + solid * f[i] + scale * (even - odd)
-                hot = functools.reduce(jnp.add, heat)
-                for i in range(7):
-                    share = hot * (HEAT_WEIGHT[i] / TAU_HEAT)
-                    if i > 0:
-                        d = [abs(v) for v in FLOW[i]].index(1)
-                        sign = FLOW[i][d]
-                        share = share * (1.0 + (4.0 * sign) * u[d])
-                    out[19 + i] = (1.0 - 1.0 / TAU_HEAT) * heat[i] + share
+                if part != "heat":
+                    solid = solid_ref[z, :, cols]
+                    flat = 1.0 - 1.5 * (u[0] * u[0] + u[1] * u[1] + u[2] * u[2])
+                    fluid = 1.0 - solid
+                    keep = fluid * (1.0 - 1.0 / TAU_FLOW)
+                    gain = fluid * rho * (1.0 / TAU_FLOW)
+                    out[0] = (keep + solid) * f[0] + gain * WEIGHT[0] * flat
+                    for i in range(1, 19, 2):
+                        along = None
+                        for d in range(3):
+                            if FLOW[i][d] == 1:
+                                along = u[d] if along is None else along + u[d]
+                            elif FLOW[i][d] == -1:
+                                along = -u[d] if along is None else along - u[d]
+                        even = flat + 4.5 * along * along
+                        odd = 3.0 * along
+                        scale = gain * WEIGHT[i]
+                        out[i] = keep * f[i] + solid * f[i + 1] + scale * (even + odd)
+                        out[i + 1] = keep * f[i + 1] + solid * f[i] + scale * (even - odd)
+                if part != "flow":
+                    hot = functools.reduce(jnp.add, heat)
+                    for i in range(7):
+                        share = hot * (HEAT_WEIGHT[i] / TAU_HEAT)
+                        if i > 0:
+                            d = [abs(v) for v in FLOW[i]].index(1)
+                            sign = FLOW[i][d]
+                            share = share * (1.0 + (4.0 * sign) * u[d])
+                        out[19 + i] = (1.0 - 1.0 / TAU_HEAT) * heat[i] + share
                 for i in range(26):
-                    ez = EVERY[i][2]
+                    if out[i] is None:
+                        continue
+                    ex, ez = EVERY[i][0], EVERY[i][2]
                     post[i, z, :, cols] = out[i]
                     if ez == 1 and z == 1:
                         zs[step, 0, Z_UP.index(i), :, cols] = out[i]
                     if ez == -1 and z == 0:
                         zs[step, 1, Z_DOWN.index(i), :, cols] = out[i]
-                    if EVERY[i][0] == 1:
-                        r = X_UP.index(i) * 2 + z
-                        xs[step, 0, r : r + 1, cols] = out[i][7:8, :]
-                    if EVERY[i][0] == -1:
-                        r = X_DOWN.index(i) * 2 + z
-                        xs[step, 1, r : r + 1, cols] = out[i][0:1, :]
+                    if ex == 0:
+                        continue
+                    way = 0 if ex == 1 else 1
+                    row = out[i][7:8, :] if ex == 1 else out[i][0:1, :]
+                    if step == 1 and i >= 19:
+                        xh_s[way, z : z + 1, cols] = row
+                    else:
+                        r = (X_UP if ex == 1 else X_DOWN).index(i) * 2 + z
+                        xs[step, way, r : r + 1, cols] = row
 
     def halo(step):
         made = []
@@ -338,14 +367,34 @@
         put(3, zs.at[step, 1, Z_DOWN.index(EDGES[3])], er.at[step, 3], g_dn, s_dn)
         put(4, xs.at[step, 0], xr.at[step, 0], g_up, si)
         put(5, xs.at[step, 1], xr.at[step, 1], g_dn, si)
-        put(6, zs.at[step, 0], zr.at[step, 0], gi, s_up)
-        put(7, zs.at[step, 1], zr.at[step, 1], gi, s_dn)
+        count = 6 if step == 0 else 5
+        put(6, zs.at[step, 0, 0:count], zr.at[step, 0, 0:count], gi, s_up)
+        put(7, zs.at[step, 1, 0:count], zr.at[step, 1, 0:count], gi, s_dn)
         return made
 
+    def heat_halo():
+        pairs = (
+            (xh_s.at[0], xh_r.at[0], g_up, si),
+            (xh_s.at[1], xh_r.at[1], g_dn, si),
+            (zs.at[1, 0, 5], zr.at[1, 0, 5], gi, s_up),
+            (zs.at[1, 1, 5], zr.at[1, 1, 5], gi, s_dn),
+        )
+        return [
+            pltpu.make_async_remote_copy(
+                src_ref=src,
+                dst_ref=dst,
+                send_sem=heat_send.at[n],
+                recv_sem=heat_recv.at[n],
+                device_id=(a, b),
+                device_id_type=MESH,
+            )
+            for n, (src, dst, a, b) in enumerate(pairs)
+        ]
+
     edge8 = iota((8, CY), 0)
 
-    def stream(step, arrived):
-        for i in range(26):
+    def stream(step, arrived, which=range(26)):
+        for i in which:
             ex, ey, ez = EVERY[i]
             for z in range(2):
                 edge = None
@@ -355,12 +404,13 @@
                 if ez == 0 or (ez == 1 and z == 1) or (ez == -1 and z == 0):
                     source = z - ez
                     piece = post[i, source]
-                    if ex == 1:
-                        r = X_UP.index(i) * 2 + source
-                        edge = xr[step, 0, r : r + 1, :]
-                    if ex == -1:
-                        r = X_DOWN.index(i) * 2 + source
-                        edge = xr[step, 1, r : r + 1, :]
+                    if ex != 0:
+                        way = 0 if ex == 1 else 1
+                        if step == 1 and i >= 19:
+                            edge = xh_r[way, source : source + 1, :]
+                        else:
+                            r = (X_UP if ex == 1 else X_DOWN).index(i) * 2 + source
+                            edge = xr[step, way, r : r + 1, :]
                 else:
                     if ez == 1:
                         piece = zr[step, 0, Z_UP.index(i)]
@@ -380,47 +430,49 @@
                     piece = pltpu.roll(piece, CY - 1, 1)
                 cur[i, z] = piece
 
-    collide(0)
+    collide(0, "all")
     pl.semaphore_wait(barrier, 8)
     made = halo(0)
     for c in made:
         c.start()
     tell(0)
     stream(0, False)
-    slot_tables()
     hear(0)
     tell(1)
     row_tables()
     hear(1)
     tell(2)
-    coupling_tables()
+    slot_tables()
     hear(2)
     tell(3)
-    code_tables()
+    fetch.wait()
+    coupling_tables()
     for c in made:
         c.wait_recv()
     stream(0, True)
-    collide(1)
+    collide(1, "heat")
+    warm = heat_halo()
+    for c in warm:
+        c.start()
+    collide(1, "flow")
     made = halo(1)
     for c in made:
         c.start()
-    stream(1, False)
+    stream(1, False, range(19, 26))
+    stream(1, False, range(19))
+    code_tables()
     x0 = start_ref[0]
     fixed = source_ref[0] + off_diagonal(x0)
     diag = diag_ref[0]
-    for c in made:
+    for c in warm:
         c.wait_recv()
-    stream(1, True)
+    stream(1, True, range(19, 26))
 
     hot_rows = []
     for z in range(2):
         hot = functools.reduce(jnp.add, [cur[19 + i, z] for i in range(7)])
         temp_out[z] = hot
         hot_rows.append(hot)
-        for d in range(3):
-            pos = [cur[i, z] for i in range(19) if FLOW[i][d] == 1]
-            neg = [cur[i, z] for i in range(19) if FLOW[i][d] == -1]
-            motion_out[d, z] = functools.reduce(jnp.add, pos) - functools.reduce(jnp.add, neg)
 
     table = jnp.concatenate(
         [hot_rows[z][:, c * 128 : (c + 1) * 128] for c in range(3) for z in range(2)], axis=0
@@ -486,6 +538,15 @@
     lax.fori_loop(0, 2 * half, near, 0)
     landed[j * groups + g] = laid_out[si]
 
+    for c in made:
+        c.wait_recv()
+    stream(1, True, range(19))
+    for z in range(2):
+        for d in range(3):
+            pos = [cur[i, z] for i in range(19) if FLOW[i][d] == 1]
+            neg = [cur[i, z] for i in range(19) if FLOW[i][d] == -1]
+            motion_out[d, z] = functools.reduce(jnp.add, pos) - functools.reduce(jnp.add, neg)
+
     early = si // (subs // 2)
     for way in (early, 1 - early):
         pltpu.make_async_copy(block_out.at[way], block_in.at[way], block_recv.at[way]).wait()
@@ -536,7 +597,7 @@
     values = dot(coded, ecode[...], ((1,), (0,)))
     values = jnp.concatenate([values[:, k * 128 : (k + 1) * 128] for k in range(16)], axis=0)
     values = (values * mask[...]).astype(BF16)
-    summed = dot(values, lohot[...], ((0,), (0,)))
+    summed = dot(lohot_t[...], values, ((1,), (0,))).T
     add_source = summed[0:8] + summed[32:40] + summed[64:72]
     add_diag = summed[8:16] + summed[40:48] + summed[72:80]
 
@@ -619,6 +680,8 @@
     for step in range(STEPS):
         for c in halo(step):
             c.wait_send()
+    for c in warm:
+        c.wait_send()
     block_copy(0).wait_send()
     block_copy(1).wait_send()
     strip_all(0, strip_send).wait()
@@ -662,7 +725,7 @@
         made = pl.pallas_call(
             functools.partial(kernel, groups, bands),
             out_shape=tuple(pltpu.VMEM(v.shape, v.dtype) for v in shapes),
-            in_specs=[vmem] * 9 + [smem] + [vmem] * 2,
+            in_specs=[vmem] * 8 + [pl.BlockSpec(memory_space=pl.ANY), smem] + [vmem] * 2,
             out_specs=(vmem,) * 4,
             scratch_shapes=[
                 pltpu.VMEM((26, 2, 8, CY), F32),
@@ -675,6 +738,10 @@
                 pltpu.VMEM((1024, 256), BF16),
                 pltpu.VMEM((1024, 256), BF16),
                 pltpu.VMEM((1024, 128), BF16),
+                pltpu.VMEM((128, 1024), BF16),
+                *[pltpu.VMEM((2, 8, CY), F32)] * 2,
+                pltpu.VMEM((4, 2, 8, CY), F32),
+                pltpu.VMEM((8, 128, 128), F32),
                 pltpu.VMEM((1024, 128), F32),
                 pltpu.VMEM((128, 512), F32),
                 pltpu.VMEM((64, 512), BF16),
@@ -694,6 +761,9 @@
                 dma,
                 dma((2,)),
                 dma((2,)),
+                dma((4,)),
+                dma((4,)),
+                dma,
                 pltpu.SemaphoreType.REGULAR((4,)),
             ],
             compiler_params=pltpu.CompilerParams(collective_id=0, has_side_effects=True),

time: 67.9 us -> 67 us (0.987)
  Pallas kernels: 67.1 us -> 66.2 us
    pallas_call x1, Pallas kernels: 66.5 us -> 65.6 us  [body(): pl.pallas_call(functools.partial(kernel, groups, bands), out_shape=tuple(...]
where the time goes in v5:
time: 67 us; the launch traced here: 66.8 us
  Pallas kernels  66.2 us (99%)
    pallas_call x1, Pallas kernels, body(): pl.pallas_call(functools.partial(kernel, groups, bands), out_shape=tuple(...  65.6 us

profile of v5, /device:TPU:1, one launch (start us, length us, event | category | flops | bytes accessed | tf_op | source)
XLA Modules:
  0.0 66.8 jit_solution(17134273911093731978)
XLA Ops:
  0.6 65.6 %coupled_step.1 = (f32[2,8,384]{2,1,0:T(8,128)S(1)}, f32[3,2,8,384]{3,2,1,0:T(8,128)S(1)}, f32[1,8,128]{2,1,0:T(8,128)S(1)}, f32[1,512]{1,0:T(1,128)S(1)}) custom-call(f32[19,2,8,384]{3,2,1,0:T(8,128)} %pops_ref.1, f32[7,2,8,384]{3,2,1,0:T(8,128)} %heat_ref.1, f32[2,8,384]{2,1,0:T(8,128)} %solid_ref.1, s32[1,512]{1,0:T(1,128)} %voxel_ref.1, ...), custom_call_target="tpu_custom_call" | custom-call | tf_op jit(solution)/shard_map/coupled_step/pallas_call | solution.py:725
  66.2 0.6 publish.1

commit v6 on v5

--- a/solution.py
+++ b/solution.py
@@ -122,6 +122,8 @@
     landed,
     returned,
     received,
+    mom_s,
+    mom_r,
     tot,
     rtot,
     halo_send,
@@ -135,6 +137,8 @@
     heat_send,
     heat_recv,
     coup_sem,
+    mom_send,
+    mom_recv,
     ready,
 ):
     subs = groups * 8
@@ -262,11 +266,14 @@
         out = dot(both, table[...], ((1,), (0,)))
         return out[0:8, 0:128] + out[8:16, 0:128] + out[0:8, 128:256]
 
-    def off_diagonal(v):
+    def by_partner(v):
         partner = jnp.zeros((8, 128), F32)
         for k in range(8):
             partner = jnp.where(pat_col == k, v[k : k + 1, :], partner)
-        forward = block_dot(partner, cthop)
+        return block_dot(partner, cthop)
+
+    def off_diagonal(v):
+        forward = by_partner(v)
         terms = block_dot(v, chop)
         backward = jnp.zeros((8, 128), F32)
         for b in range(8):
@@ -568,8 +575,7 @@
         lax.fori_loop(0, half - 1, forward_all, 0)
 
     def back_copy(i):
-        d = subs // 2 + (1 - 2 * (i % 2)) * ((i + 1) // 2)
-        to = lax.rem(si + d, subs)
+        to = far_first(i)
         return pltpu.make_async_remote_copy(
             src_ref=returned.at[(to % 8) * groups + to // 8],
             dst_ref=received.at[si],
@@ -604,8 +610,36 @@
     diag = diag + add_diag
     r0 = fixed + add_source - diag * x0
     w1 = (diag - SHIFT) * r0 - off_diagonal(r0)
-    w2 = (diag - SHIFT) * w1 - off_diagonal(w1)
-    sums = [total(r0 * r0), total(r0 * w1), total(w1 * w1), total(w1 * w2)]
+    last = (diag - SHIFT) * w1 - 2.0 * by_partner(w1)
+    sums = [total(r0 * r0), total(r0 * w1), total(w1 * w1), total(w1 * last)]
+
+    lane1 = iota((1, 128), 1)
+    line = jnp.zeros((1, 128), F32)
+    for n in range(4):
+        line = jnp.where(lane1 == 48 + n, sums[n], line)
+    mom_s[...] = line
+
+    def far_first(i):
+        d = subs // 2 + (1 - 2 * (i % 2)) * ((i + 1) // 2)
+        return lax.rem(si + d, subs)
+
+    def mom_go(i, carry):
+        pltpu.make_async_remote_copy(
+            src_ref=mom_s,
+            dst_ref=mom_r.at[si],
+            send_sem=mom_send,
+            recv_sem=mom_recv,
+            device_id=(gi, far_first(i)),
+            device_id_type=MESH,
+        ).start()
+        return carry
+
+    lax.fori_loop(0, subs - 1, mom_go, 0)
+    mom_r[si] = line
+
+    def mom_all(sem):
+        rest = pl.ds(0, subs - 1)
+        return pltpu.make_async_copy(landed.at[rest], mom_r.at[rest], sem)
 
     held = jnp.concatenate([x0, r0, w1, jnp.zeros((8, 128), F32)], axis=0)
     held = jnp.concatenate(list(parts3(held)) + [jnp.zeros((32, 128), F32)], axis=0).astype(BF16)
@@ -613,14 +647,11 @@
     found = (found * mask[...]).astype(BF16)
     found = jnp.concatenate([found[k * 64 : (k + 1) * 64, :] for k in range(16)], axis=1)
     found = dot(found, fcode[...], ((1,), (0,)))
-    for n in range(4):
-        found = jnp.where(lane == 48 + n, sums[n], found)
     returned[...] = found.reshape(64, 1, 128)
     lax.fori_loop(0, subs - 1, back_go, 0)
     received[si] = returned[j * groups + g]
-    strip_all(1, strip_recv).wait()
-    back = received[...].reshape(64, 128)
-    tot[...] = jnp.sum(back, axis=0, keepdims=True)
+    mom_all(mom_recv).wait()
+    tot[...] = jnp.sum(mom_r[...].reshape(64, 128), axis=0, keepdims=True)
 
     def band_copy(i):
         return pltpu.make_async_remote_copy(
@@ -642,7 +673,8 @@
         rest = pl.ds(0, bands - 1)
         return pltpu.make_async_copy(laid_out.at[rest], rtot.at[rest], sem)
 
-    back = jnp.where(lane < 48, back, 0.0)
+    strip_all(1, strip_recv).wait()
+    back = received[...].reshape(64, 128)
     rows = functools.reduce(
         jnp.add, [dot(p.astype(BF16), dhot[...], ((0,), (0,))) for p in parts3(back)]
     )
@@ -654,7 +686,6 @@
     rtot[gi] = tot[...]
 
     band_all(band_recv).wait()
-    lane1 = iota((1, 128), 1)
     whole = functools.reduce(jnp.add, [rtot[n] for n in range(bands)])
 
     def lane_value(n):
@@ -687,6 +718,7 @@
     strip_all(0, strip_send).wait()
     strip_all(1, strip_send).wait()
     band_all(band_send).wait()
+    mom_all(mom_send).wait()
 
 
 def publish(*refs):
@@ -752,6 +784,8 @@
                 *[pltpu.VMEM((2, 16, 1, 128), F32)] * 2,
                 *[pltpu.VMEM((64, 1, 128), F32)] * 3,
                 pltpu.VMEM((1, 128), F32),
+                pltpu.VMEM((64, 1, 128), F32),
+                pltpu.VMEM((1, 128), F32),
                 pltpu.VMEM((bands, 1, 128), F32),
                 dma((STEPS, 8)),
                 dma((STEPS, 8)),
@@ -763,6 +797,8 @@
                 dma((2,)),
                 dma((4,)),
                 dma((4,)),
+                dma,
+                dma,
                 dma,
                 pltpu.SemaphoreType.REGULAR((4,)),
             ],

time: 67 us -> 66.7 us (level)
  no operation moved by 1% of the time
where the time goes in v6:
time: 66.7 us; the launch traced here: 66.5 us
  Pallas kernels  65.9 us (99%)
    pallas_call x1, Pallas kernels, body(): pl.pallas_call(functools.partial(kernel, groups, bands), out_shape=tuple(...  65.2 us

profile of v6, /device:TPU:1, one launch (start us, length us, event | category | flops | bytes accessed | tf_op | source)
XLA Modules:
  0.0 66.5 jit_solution(9681144785988077480)
XLA Ops:
  0.6 65.2 %coupled_step.1 = (f32[2,8,384]{2,1,0:T(8,128)S(1)}, f32[3,2,8,384]{3,2,1,0:T(8,128)S(1)}, f32[1,8,128]{2,1,0:T(8,128)S(1)}, f32[1,512]{1,0:T(1,128)S(1)}) custom-call(f32[19,2,8,384]{3,2,1,0:T(8,128)} %pops_ref.1, f32[7,2,8,384]{3,2,1,0:T(8,128)} %heat_ref.1, f32[2,8,384]{2,1,0:T(8,128)} %solid_ref.1, s32[1,512]{1,0:T(1,128)} %voxel_ref.1, ...), custom_call_target="tpu_custom_call" | custom-call | tf_op jit(solution)/shard_map/coupled_step/pallas_call | solution.py:757
  65.9 0.6 publish.1

commit v7 on v6

--- a/solution.py
+++ b/solution.py
@@ -659,7 +659,7 @@
             dst_ref=rtot.at[gi],
             send_sem=band_send,
             recv_sem=band_recv,
-            device_id=(lax.rem(gi + i, bands), si),
+            device_id=(lax.rem(gi + bands // 2 + (1 - 2 * (i % 2)) * ((i + 1) // 2), bands), si),
             device_id_type=MESH,
         )
 
@@ -667,7 +667,7 @@
         band_copy(i).start()
         return carry
 
-    lax.fori_loop(1, bands, band_go, 0)
+    lax.fori_loop(0, bands - 1, band_go, 0)
 
     def band_all(sem):
         rest = pl.ds(0, bands - 1)

time: 66.7 us -> 66.9 us (level)
  no operation moved by 1% of the time
where the time goes in v7:
time: 66.9 us; the launch traced here: 66.8 us
  Pallas kernels  66.1 us (99%)
    pallas_call x1, Pallas kernels, body(): pl.pallas_call(functools.partial(kernel, groups, bands), out_shape=tuple(...  65.5 us

profile of v7, /device:TPU:1, one launch (start us, length us, event | category | flops | bytes accessed | tf_op | source)
XLA Modules:
  0.0 66.8 jit_solution(664878353319560163)
XLA Ops:
  0.6 65.5 %coupled_step.1 = (f32[2,8,384]{2,1,0:T(8,128)S(1)}, f32[3,2,8,384]{3,2,1,0:T(8,128)S(1)}, f32[1,8,128]{2,1,0:T(8,128)S(1)}, f32[1,512]{1,0:T(1,128)S(1)}) custom-call(f32[19,2,8,384]{3,2,1,0:T(8,128)} %pops_ref.1, f32[7,2,8,384]{3,2,1,0:T(8,128)} %heat_ref.1, f32[2,8,384]{2,1,0:T(8,128)} %solid_ref.1, s32[1,512]{1,0:T(1,128)} %voxel_ref.1, ...), custom_call_target="tpu_custom_call" | custom-call | tf_op jit(solution)/shard_map/coupled_step/pallas_call | solution.py:757
  66.1 0.6 publish.1
